TPU v7x, 32 devices: a whole 2x2x4 slice. The times are simulated.
32 devices in a mesh: section: 4 (over z), tensor: 8 (over y, x, core).
Axes of the slice: x: 2, y: 2, z: 4, core: 2. Of those that a mesh axis runs over, the one named last changes fastest.
Arguments:
- resid: bfloat16 [32, 3584], P('tensor'), may hold values from -6 to 6
- w_enc: bfloat16 [7168, 3584], P(('section', 'tensor')), may hold values from -0.09375 to 0.09375
- b_enc: float32 [7168], P(('section', 'tensor')), may hold values from -1 to 0.5
- w_dec: bfloat16 [7168, 3584], P(('section', 'tensor')), may hold values from -0.0625 to 0.0625
- b_dec: float32 [3584], replicated, may hold values from -3 to 3
Outputs:
- recon: float32 [32, 3584], P('tensor')
- grad_w_dec: bfloat16 [7168, 3584], P(('section', 'tensor'))
- code_grad: float32 [32, 7168], P(None, ('section', 'tensor'))
- grad_b_dec: float32 [3584], replicated
- loss_value: float32 [], replicated
All inputs are finite; a program needn't handle non-finite values.
Results may differ from a plain program's by a relative error of at most 0.0032.
The roundings to bfloat16 on the way count: a program that leaves them out, or rounds other values in their place, can miss the bound.
Values may be sent and summed in bfloat16 or wider, within the bound.
No kernel may reach another device: no remote copies, remote signals or barrier semaphores. Data moves between devices by JAX's collectives and lax.ppermute only.
A program may use at most 64 MiB of HBM per device.

v0:
```python
import functools

import jax
import jax.numpy as jnp
from jax import lax
from jax.experimental import pallas as pl
from jax.experimental.pallas import tpu as pltpu
from jax.sharding import PartitionSpec as P


epsilon = 1e-06
LANES = 128


BF16, F32 = jnp.bfloat16, jnp.float32
VMEM = pl.BlockSpec(memory_space=pltpu.VMEM)
PARAMS = pltpu.CompilerParams(vmem_limit_bytes=16 << 20)


def swap(x, axis, size, mask):
    return lax.ppermute(x, axis, [(i, i ^ mask) for i in range(size)])


def swaps(xs, axis, size, masks):
    out = []
    for x, m in zip(xs, masks):
        out.append(swap(x, axis, size, m))
    return out


def far_masks(size):
    return [0] + list(range(3, size, 2))


def tree_sum(terms):
    while len(terms) > 1:
        terms = [terms[i] + terms[i + 1] for i in range(0, len(terms), 2)]
    return terms[0]


def chunk_of(width):
    return next(c for c in (512, 384, 256, 128) if width % c == 0)


def contract(a, b, dims):
    return lax.dot_general(a, b, (dims, ((), ())), preferred_element_type=F32)


def prepare_kernel(dec_ref, bias_ref, resid_ref, norm_ref, bias_col_ref, own_ref):
    lat, width = dec_ref.shape
    total = jnp.zeros((lat, LANES), F32)
    for c in range(0, width, LANES):
        part = dec_ref[:, c : c + LANES].astype(F32)
        total = total + part * part
    norm_ref[...] = jnp.sqrt(jnp.sum(total, axis=1, keepdims=True) + epsilon)
    bias_col_ref[...] = jnp.transpose(jnp.broadcast_to(bias_ref[...], (8, lat)))[:, :1]
    own_ref[...] = resid_ref[...]


def forward_kernel(
    near_ref, other_ref, enc_ref, bias_ref, dec_ref, norm_ref,
    keep_ref, send_ref, codes_ref, scale_ref, rows_f32,
):
    half, rows, width = near_ref.shape
    for p in range(2 * half):
        block = near_ref[p] if p < half else other_ref[p - half]
        rows_f32[p * rows : (p + 1) * rows, :] = block.astype(F32)
    stream = rows_f32[...].astype(BF16)
    preact = contract(enc_ref[...], stream, ((1,), (1,))) + bias_ref[...]
    codes = jnp.maximum(preact, 0.0).astype(BF16)
    codes_ref[...] = codes
    codes_f32 = codes.astype(F32)
    norm = norm_ref[...]
    scale_ref[...] = jnp.sum(codes_f32, axis=1, keepdims=True) / norm
    penalty = jnp.sum(codes_f32 * norm, axis=(0, 1), keepdims=True)
    tail = jnp.broadcast_to(penalty, (rows, LANES))
    by_row = jnp.transpose(codes_f32).astype(BF16)
    for out_ref in (keep_ref, send_ref):
        for k in range(half):
            out_ref[k, :, width:] = tail
    chunk = chunk_of(width)
    for c in range(0, width, chunk):
        part = contract(by_row, dec_ref[:, c : c + chunk], ((1,), (0,)))
        for p in range(2 * half):
            out_ref = keep_ref if p < half else send_ref
            out_ref[p % half, :, c : c + chunk] = part[p * rows : (p + 1) * rows]


def error_kernel(n_tensor, n_terms, *refs):
    terms, (bias_ref, resid_ref, recon_ref, out_ref, pack) = refs[:n_terms], refs[n_terms:]
    rows, width = resid_ref.shape
    cut, piece = width // 2, width // rows
    total = tree_sum([t[...] for t in terms])
    recon = total[:, :width] + bias_ref[...]
    recon_ref[...] = recon
    errors = recon - resid_ref[...].astype(F32)
    column = jnp.sum(errors, axis=0, keepdims=True)
    squares = jnp.sum(errors * errors, axis=(0, 1), keepdims=True)
    value = 0.5 * squares + total[:1, width : width + 1] * (1.0 / n_tensor)
    pack[:rows, :cut] = errors[:, :cut]
    pack[rows:, :cut] = errors[:, cut:]
    high = column.astype(BF16).astype(F32)
    low = column - high
    for r in range(rows):
        pack[r : r + 1, cut : cut + piece] = high[:, r * piece : (r + 1) * piece]
        pack[rows + r : rows + r + 1, cut : cut + piece] = low[:, r * piece : (r + 1) * piece]
    pack[:, cut + piece :] = jnp.zeros((2 * rows, LANES), F32)
    for r in range(3):
        high = value.astype(BF16).astype(F32)
        pack[r : r + 1, cut + piece :] = jnp.broadcast_to(high, (1, LANES))
        value = value - high
    out_ref[...] = pack[...].astype(BF16)


def backward_kernel(
    order, near_ref, other_ref, codes_ref, scale_ref, dec_ref, norm_ref,
    grad_ref, code_grad_ref, column_ref, loss_ref, rows_f32, staged, sems,
):
    half, rows2, _ = near_ref.shape
    rows = rows2 // 2
    _, width = dec_ref.shape
    cut, piece = width // 2, width // rows
    columns, losses = {}, {}
    for p, mask in enumerate(order):
        block = (near_ref[p] if p < half else other_ref[p - half]).astype(F32)
        rows_f32[p * rows : (p + 1) * rows, :cut] = block[:rows, :cut]
        rows_f32[p * rows : (p + 1) * rows, cut:] = block[rows:, :cut]
        columns[mask] = block[:rows, cut : cut + piece] + block[rows:, cut : cut + piece]
        ends = block[:, cut + piece : cut + piece + 1]
        losses[mask] = (ends[0:1] + ends[1:2]) + ends[2:3]
    errors = rows_f32[...].astype(BF16)
    codes, scale = codes_ref[...], scale_ref[...]
    chunk = staged.shape[2]
    copies = []
    for i in range(width // chunk):
        cols = slice(i * chunk, (i + 1) * chunk)
        grad = contract(codes, errors[:, cols], ((1,), (0,)))
        staged[i] = (grad + scale * dec_ref[:, cols].astype(F32)).astype(BF16)
        copies.append(pltpu.make_async_copy(staged.at[i], grad_ref.at[:, cols], sems.at[i]))
        copies[-1].start()
    by_lat = contract(dec_ref[...], errors, ((1,), (1,))) + norm_ref[...]
    by_row = jnp.transpose(by_lat)
    me = lax.axis_index("tensor")
    for p, mask in enumerate(order[:half]):
        block = lax.bitwise_xor(me, mask)
        one = by_row[p * rows : (p + 1) * rows]
        two = by_row[(half + p) * rows : (half + p + 1) * rows]
        if len(code_grad_ref.shape) == 3:
            code_grad_ref[block] = one
            code_grad_ref[lax.bitwise_xor(block, 1)] = two
        else:
            odd = lax.rem(block, 2) == 1
            both = jnp.concatenate([jnp.where(odd, two, one), jnp.where(odd, one, two)])
            start = pl.multiple_of(lax.div(block, 2) * 2 * rows, 2 * rows)
            code_grad_ref[pl.ds(start, 2 * rows), :] = both
    column = tree_sum([columns[m] for m in range(len(order))])
    for r in range(rows):
        column_ref[r * piece : (r + 1) * piece] = column[r]
    loss_ref[...] = tree_sum([losses[m] for m in range(len(order))]) / (len(order) * rows * width)
    for copy in copies:
        copy.wait()


def per_device(n_section, n_tensor, resid, w_enc, b_enc, w_dec, b_dec):
    rows, width = resid.shape
    lat = w_enc.shape[0]
    masks = far_masks(n_tensor)
    order = masks + [m ^ 1 for m in masks]
    half = len(masks)
    total_rows = n_tensor * rows
    wide = width + LANES
    shape = jax.ShapeDtypeStruct

    norm, bias, own = pl.pallas_call(
        prepare_kernel,
        out_shape=(shape((lat, 1), F32), shape((lat, 1), F32), shape((rows, width), BF16)),
        in_specs=[VMEM] * 3,
        out_specs=(VMEM,) * 3,
        compiler_params=PARAMS,
    )(w_dec, b_enc.reshape(1, lat), resid)
    near = jnp.stack([own] + swaps([resid] * half, "tensor", n_tensor, masks[1:]))
    near, norm, bias = lax.optimization_barrier((near, norm, bias))
    other = swap(near, "tensor", n_tensor, 1)
    keep, send, codes, scale = pl.pallas_call(
        forward_kernel,
        out_shape=(
            shape((half, rows, wide), F32),
            shape((half, rows, wide), F32),
            shape((lat, total_rows), BF16),
            shape((lat, 1), F32),
        ),
        in_specs=[VMEM] * 6,
        out_specs=(VMEM,) * 4,
        compiler_params=PARAMS,
        scratch_shapes=[pltpu.VMEM((total_rows, width), F32)],
    )(near, other, w_enc, bias, w_dec, norm)
    pair = keep + swap(send, "tensor", n_tensor, 1)
    share = pair[0]
    for part in swaps(list(pair[1:]), "tensor", n_tensor, masks[1:]):
        share = share + part
    across = range(1, n_section)
    terms = [share] + swaps([share] * n_section, "section", n_section, across)
    packed = width // 2 + width // rows + LANES
    recon, payload = pl.pallas_call(
        functools.partial(error_kernel, n_tensor, len(terms)),
        out_shape=(shape((rows, width), F32), shape((2 * rows, packed), BF16)),
        in_specs=[VMEM] * (len(terms) + 2),
        out_specs=(VMEM, VMEM),
        compiler_params=PARAMS,
        scratch_shapes=[pltpu.VMEM((2 * rows, packed), F32)],
    )(*terms, b_dec.reshape(1, width), own)
    near = jnp.stack([payload] + swaps([payload] * half, "tensor", n_tensor, masks[1:]))
    other = swap(near, "tensor", n_tensor, 1)
    chunk = chunk_of(width)
    grad_w_dec, code_grad, column, loss = pl.pallas_call(
        functools.partial(backward_kernel, order),
        out_shape=(
            shape((lat, width), BF16),
            shape((total_rows, lat) if rows % 4 == 0 else (n_tensor, rows, lat), F32),
            shape((width,), F32),
            shape((1, 1), F32),
        ),
        in_specs=[VMEM] * 6,
        out_specs=(pl.BlockSpec(memory_space=pl.ANY), VMEM, VMEM, VMEM),
        compiler_params=PARAMS,
        scratch_shapes=[
            pltpu.VMEM((total_rows, width), F32),
            pltpu.VMEM((width // chunk, lat, chunk), BF16),
            pltpu.SemaphoreType.DMA((width // chunk,)),
        ],
    )(near, other, codes, scale, w_dec, norm)
    return recon, grad_w_dec, code_grad.reshape(total_rows, lat), column, loss.reshape(())


def solution(mesh):
    n_section, n_tensor = mesh.shape["section"], mesh.shape["tensor"]
    in_specs = (
        P("tensor", None),
        P(("section", "tensor"), None),
        P(("section", "tensor")),
        P(("section", "tensor"), None),
        P(),
    )
    out_specs = (
        P("tensor", None),
        P(("section", "tensor"), None),
        P(None, ("section", "tensor")),
        P(),
        P(),
    )

    def body(*args):
        return per_device(n_section, n_tensor, *args)

    return jax.shard_map(body, mesh=mesh, in_specs=in_specs, out_specs=out_specs, check_vma=False)
```

profile of v0, /device:TPU:0, one launch (start us, length us, event | category | flops | bytes accessed | tf_op | source)
XLA Modules:
  0.0 40.9 jit_solution(548435943164335682)
XLA Ops:
  0.6 2.5 %collective-permute-start = (bf16[4,3584]{1,0:T(4,128)(2,1)}, bf16[4,3584]{1,0:T(4,128)(2,1)S(1)}, u32[]{:S(2)}, u32[]{:S(2)}) collective-permute-start(bf16[4,3584]{1,0:T(4,128)(2,1)} %resid_ref.1), channel_id=1, source_target_pairs={{0,3},{1,2},{2,1},{3,0},{4,7},{5,6},{6,5},{7,4},{8,11},{9,10},{10,... | collective-permute-start | bytes 86024 | tf_op jit(solution)/shard_map/ppermute | solution.py:21
  3.1 1.8 %collective-permute-start.2 = (bf16[4,3584]{1,0:T(4,128)(2,1)}, bf16[4,3584]{1,0:T(4,128)(2,1)S(1)}, u32[]{:S(2)}, u32[]{:S(2)}) collective-permute-start(bf16[4,3584]{1,0:T(4,128)(2,1)} %resid_ref.1), channel_id=1, source_target_pairs={{0,7},{1,6},{2,5},{3,4},{4,3},{5,2},{6,1},{7,0},{8,15},{9,14},{10,... | collective-permute-start | bytes 86024 | tf_op jit(solution)/shard_map/ppermute | solution.py:21
  4.9 0.0 collective-permute-start.1
  4.9 0.0 copy-start
  4.9 1.4 %copy-done = bf16[224,3584]{1,0:T(8,128)(2,1)S(1)} copy-done((bf16[224,3584]{1,0:T(8,128)(2,1)S(1)}, bf16[224,3584]{1,0:T(8,128)(2,1)}, u32[]{:S(2)}) %copy-start) | copy-done | bytes 1605656
  6.3 0.0 copy-start.3
  6.3 0.7 %copy-done.3 = bf16[4,3584]{1,0:T(4,128)(2,1)S(1)} copy-done((bf16[4,3584]{1,0:T(4,128)(2,1)S(1)}, bf16[4,3584]{1,0:T(4,128)(2,1)}, u32[]{:S(2)}) %copy-start.3) | copy-done | bytes 28696
  7.1 0.0 copy-start.4
  7.1 0.7 %copy-done.4 = f32[224]{0:T(256)S(1)} copy-done((f32[224]{0:T(256)S(1)}, f32[224]{0:T(256)}, u32[]{:S(2)}) %copy-start.4) | copy-done | bytes 920
  7.8 0.0 copy-start.2
  7.8 0.4 %shard_map.92 = (f32[224,1]{1,0:T(8,128)S(1)}, f32[224,1]{1,0:T(8,128)S(1)}, bf16[4,3584]{1,0:T(4,128)(2,1)S(1)}) custom-call(bf16[224,3584]{1,0:T(8,128)(2,1)S(1)} %copy-done, f32[1,224]{1,0:T(1,128)S(1)} %bitcast.26, bf16[4,3584]{1,0:T(4,128)(2,1)S(1)} %copy-done.3), custom_call_target="tpu_custom_call" | custom-call | tf_op jit(solution)/shard_map/pallas_call | solution.py:174
  8.2 0.0 collective-permute-done
  8.2 0.0 collective-permute-done.2
  8.2 0.7 %collective-permute-done.1 = bf16[4,3584]{1,0:T(4,128)(2,1)S(1)} collective-permute-done((bf16[4,3584]{1,0:T(4,128)(2,1)}, bf16[4,3584]{1,0:T(4,128)(2,1)S(1)}, u32[]{:S(2)}, u32[]{:S(2)}) %collective-permute-start.1) | collective-permute-done | bytes 28704 | tf_op jit(solution)/shard_map/ppermute | solution.py:21
  9.0 0.1 pad_maximum_fusion.1.near_ref
  9.1 0.0 copy-start.5
  9.1 0.2 collective-permute-start.3
  9.3 1.2 %collective-permute-done.3.other_ref = bf16[4,4,3584]{2,1,0:T(4,128)(2,1)S(1)} collective-permute-done((bf16[4,4,3584]{2,1,0:T(4,128)(2,1)S(1)}, bf16[4,4,3584]{2,1,0:T(4,128)(2,1)S(1)}, u32[]{:S(2)}, u32[]{:S(2)}) %collective-permute-start.3) | collective-permute-done | bytes 114720 | tf_op jit(solution)/shard_map/ppermute | solution.py:21
  10.5 0.0 copy-done.2
  10.5 1.3 %shard_map.93 = (f32[4,4,3712]{2,1,0:T(4,128)S(1)}, f32[4,4,3712]{2,1,0:T(4,128)S(1)}, bf16[224,32]{1,0:T(8,128)(2,1)S(1)}, f32[224,1]{1,0:T(8,128)S(1)}) custom-call(bf16[4,4,3584]{2,1,0:T(4,128)(2,1)S(1)} %pad_maximum_fusion.1.near_ref, bf16[4,4,3584]{2,1,0:T(4,128)(2,1)S(1)} %collective-permute-done.3.other_ref, bf16[224,3584]{1,0:T(8,128)(2,1)S(1)} %copy-done.2, ...), custom_call_target="tpu_custom_call" | custom-call | tf_op jit(solution)/shard_map/pallas_call | solution.py:184
  11.8 0.0 copy-start.1
  11.8 0.2 collective-permute-start.4
  12.0 1.4 %collective-permute-done.4 = f32[4,4,3712]{2,1,0:T(4,128)S(1)} collective-permute-done((f32[4,4,3712]{2,1,0:T(4,128)S(1)}, f32[4,4,3712]{2,1,0:T(4,128)S(1)}, u32[]{:S(2)}, u32[]{:S(2)}) %collective-permute-start.4) | collective-permute-done | bytes 237600 | tf_op jit(solution)/shard_map/ppermute | solution.py:21
  13.4 0.1 add.12
  13.5 1.0 %collective-permute-start.5 = (f32[4,3712]{1,0:T(4,128)S(1)}, f32[4,3712]{1,0:T(4,128)S(1)}, u32[]{:S(2)}, u32[]{:S(2)}) collective-permute-start(f32[4,3712]{1,0:T(4,128)S(1)} %get-tuple-element.37), channel_id=1, source_target_pairs={{0,3},{1,2},{2,1},{3,0},{4,7},{5,6},{6,5},{7,4},{8,11},{9,10},{10,... | collective-permute-start | bytes 178184 | tf_op jit(solution)/shard_map/ppermute | solution.py:21
  14.5 1.2 %collective-permute-start.7 = (f32[4,3712]{1,0:T(4,128)S(1)}, f32[4,3712]{1,0:T(4,128)S(1)}, u32[]{:S(2)}, u32[]{:S(2)}) collective-permute-start(f32[4,3712]{1,0:T(4,128)S(1)} %get-tuple-element.38), channel_id=1, source_target_pairs={{0,7},{1,6},{2,5},{3,4},{4,3},{5,2},{6,1},{7,0},{8,15},{9,14},{10,... | collective-permute-start | bytes 178184 | tf_op jit(solution)/shard_map/ppermute | solution.py:21
  15.7 0.8 %collective-permute-start.6 = (f32[4,3712]{1,0:T(4,128)S(1)}, f32[4,3712]{1,0:T(4,128)S(1)}, u32[]{:S(2)}, u32[]{:S(2)}) collective-permute-start(f32[4,3712]{1,0:T(4,128)S(1)} %get-tuple-element.39), channel_id=1, source_target_pairs={{0,5},{1,4},{2,7},{3,6},{4,1},{5,0},{6,3},{7,2},{8,13},{9,12},{10,... | collective-permute-start | bytes 178184 | tf_op jit(solution)/shard_map/ppermute | solution.py:21
  16.5 1.0 %collective-permute-done.5 = f32[4,3712]{1,0:T(4,128)S(1)} collective-permute-done((f32[4,3712]{1,0:T(4,128)S(1)}, f32[4,3712]{1,0:T(4,128)S(1)}, u32[]{:S(2)}, u32[]{:S(2)}) %collective-permute-start.5) | collective-permute-done | bytes 59424 | tf_op jit(solution)/shard_map/ppermute | solution.py:21
  17.5 1.7 %collective-permute-done.7 = f32[4,3712]{1,0:T(4,128)S(1)} collective-permute-done((f32[4,3712]{1,0:T(4,128)S(1)}, f32[4,3712]{1,0:T(4,128)S(1)}, u32[]{:S(2)}, u32[]{:S(2)}) %collective-permute-start.7) | collective-permute-done | bytes 59424 | tf_op jit(solution)/shard_map/ppermute | solution.py:21
  19.1 1.7 %collective-permute-done.6 = f32[4,3712]{1,0:T(4,128)S(1)} collective-permute-done((f32[4,3712]{1,0:T(4,128)S(1)}, f32[4,3712]{1,0:T(4,128)S(1)}, u32[]{:S(2)}, u32[]{:S(2)}) %collective-permute-start.6) | collective-permute-done | bytes 59424 | tf_op jit(solution)/shard_map/ppermute | solution.py:21
  20.9 3.7 %collective-permute-start.10 = (f32[4,3712]{1,0:T(4,128)S(1)}, f32[4,3712]{1,0:T(4,128)S(1)}, u32[]{:S(2)}, u32[]{:S(2)}) collective-permute-start(f32[4,3712]{1,0:T(4,128)S(1)} %fusion.2.refs_0_), channel_id=1, source_target_pairs={{0,24},{8,16},{16,8},{24,0},{1,25},{9,17},{17,9},{25,1},{2,26},{10... | collective-permute-start | bytes 178184 | tf_op jit(solution)/shard_map/ppermute | solution.py:21
  24.6 0.0 collective-permute-start.9
  24.6 0.8 %collective-permute-start.8 = (f32[4,3712]{1,0:T(4,128)S(1)}, f32[4,3712]{1,0:T(4,128)S(1)}, u32[]{:S(2)}, u32[]{:S(2)}) collective-permute-start(f32[4,3712]{1,0:T(4,128)S(1)} %fusion.2.refs_0_), channel_id=1, source_target_pairs={{0,8},{8,0},{16,24},{24,16},{1,9},{9,1},{17,25},{25,17},{2,10},{10... | collective-permute-start | bytes 178184 | tf_op jit(solution)/shard_map/ppermute | solution.py:21
  25.4 0.0 copy-done.5
  25.4 1.7 %collective-permute-done.10.refs_3_ = f32[4,3712]{1,0:T(4,128)S(1)} collective-permute-done((f32[4,3712]{1,0:T(4,128)S(1)}, f32[4,3712]{1,0:T(4,128)S(1)}, u32[]{:S(2)}, u32[]{:S(2)}) %collective-permute-start.10) | collective-permute-done | bytes 59424 | tf_op jit(solution)/shard_map/ppermute | solution.py:21
  27.0 2.9 %collective-permute-done.9.refs_2_ = f32[4,3712]{1,0:T(4,128)S(1)} collective-permute-done((f32[4,3712]{1,0:T(4,128)S(1)}, f32[4,3712]{1,0:T(4,128)S(1)}, u32[]{:S(2)}, u32[]{:S(2)}) %collective-permute-start.9) | collective-permute-done | bytes 59424 | tf_op jit(solution)/shard_map/ppermute | solution.py:21
  30.0 0.0 collective-permute-done.8.refs_1_
  30.0 0.7 %shard_map.94 = (f32[4,3584]{1,0:T(4,128)}, bf16[8,2816]{1,0:T(8,128)(2,1)S(1)}) custom-call(f32[4,3712]{1,0:T(4,128)S(1)} %fusion.2.refs_0_, f32[4,3712]{1,0:T(4,128)S(1)} %collective-permute-done.8.refs_1_, f32[4,3712]{1,0:T(4,128)S(1)} %collective-permute-done.9.refs_2_, f32[4,3712]{1,0:T(4,128)S(1)} %collective-permute-done.10.refs_3_, ...), custom_call_target="tpu_custom_call" | custom-call | tf_op jit(solution)/shard_map/pallas_call | solution.py:204
  30.7 0.9 %collective-permute-start.13 = (bf16[8,2816]{1,0:T(8,128)(2,1)S(1)}, bf16[8,2816]{1,0:T(8,128)(2,1)S(1)}, u32[]{:S(2)}, u32[]{:S(2)}) collective-permute-start(bf16[8,2816]{1,0:T(8,128)(2,1)S(1)} %get-tuple-element.30), channel_id=1, source_target_pairs={{0,7},{1,6},{2,5},{3,4},{4,3},{5,2},{6,1},{7,0},{8,15},{9,14},{10,... | collective-permute-start | bytes 135176 | tf_op jit(solution)/shard_map/ppermute | solution.py:21
  31.6 1.5 %collective-permute-start.12 = (bf16[8,2816]{1,0:T(8,128)(2,1)S(1)}, bf16[8,2816]{1,0:T(8,128)(2,1)S(1)}, u32[]{:S(2)}, u32[]{:S(2)}) collective-permute-start(bf16[8,2816]{1,0:T(8,128)(2,1)S(1)} %get-tuple-element.30), channel_id=1, source_target_pairs={{0,5},{1,4},{2,7},{3,6},{4,1},{5,0},{6,3},{7,2},{8,13},{9,12},{10,... | collective-permute-start | bytes 135176 | tf_op jit(solution)/shard_map/ppermute | solution.py:21
  33.1 0.2 collective-permute-start.11
  33.3 2.3 %collective-permute-done.13 = bf16[8,2816]{1,0:T(8,128)(2,1)S(1)} collective-permute-done((bf16[8,2816]{1,0:T(8,128)(2,1)S(1)}, bf16[8,2816]{1,0:T(8,128)(2,1)S(1)}, u32[]{:S(2)}, u32[]{:S(2)}) %collective-permute-start.13) | collective-permute-done | bytes 45088 | tf_op jit(solution)/shard_map/ppermute | solution.py:21
  35.6 0.8 %collective-permute-done.12 = bf16[8,2816]{1,0:T(8,128)(2,1)S(1)} collective-permute-done((bf16[8,2816]{1,0:T(8,128)(2,1)S(1)}, bf16[8,2816]{1,0:T(8,128)(2,1)S(1)}, u32[]{:S(2)}, u32[]{:S(2)}) %collective-permute-start.12) | collective-permute-done | bytes 45088 | tf_op jit(solution)/shard_map/ppermute | solution.py:21
  36.4 0.7 %collective-permute-done.11 = bf16[8,2816]{1,0:T(8,128)(2,1)S(1)} collective-permute-done((bf16[8,2816]{1,0:T(8,128)(2,1)S(1)}, bf16[8,2816]{1,0:T(8,128)(2,1)S(1)}, u32[]{:S(2)}, u32[]{:S(2)}) %collective-permute-start.11) | collective-permute-done | bytes 45088 | tf_op jit(solution)/shard_map/ppermute | solution.py:21
  37.1 0.2 collective-permute-start.14
  37.2 1.3 %collective-permute-done.14.other_ref = bf16[4,8,2816]{2,1,0:T(8,128)(2,1)S(1)} collective-permute-done((bf16[4,8,2816]{2,1,0:T(8,128)(2,1)S(1)}, bf16[4,8,2816]{2,1,0:T(8,128)(2,1)S(1)}, u32[]{:S(2)}, u32[]{:S(2)}) %collective-permute-start.14) | collective-permute-done | bytes 180256 | tf_op jit(solution)/shard_map/ppermute | solution.py:21
  38.5 0.0 copy-done.1
  38.6 2.3 %shard_map.95 = (bf16[224,3584]{1,0:T(8,128)(2,1)}, f32[32,224]{1,0:T(8,128)}, f32[3584]{0:T(1024)}, f32[1,1]{1,0:T(1,128)}) custom-call(bf16[4,8,2816]{2,1,0:T(8,128)(2,1)S(1)} %pad_maximum_fusion.near_ref, bf16[4,8,2816]{2,1,0:T(8,128)(2,1)S(1)} %collective-permute-done.14.other_ref, bf16[224,32]{1,0:T(8,128)(2,1)S(1)} %get-tuple-element.31.codes_ref, ...), custom_call_target="tpu_custom_call" | custom-call | tf_op jit(solution)/shard_map/pallas_call | solution.py:215
  (4 shorter events, 0.1 us)
Async XLA Ops:
  0.6 7.6 %collective-permute-start = (bf16[4,3584]{1,0:T(4,128)(2,1)}, bf16[4,3584]{1,0:T(4,128)(2,1)S(1)}, u32[]{:S(2)}, u32[]{:S(2)}) collective-permute-start(bf16[4,3584]{1,0:T(4,128)(2,1)} %resid_ref.1), channel_id=1, source_target_pairs={{0,3},{1,2},{2,1},{3,0},{4,7},{5,6},{6,5},{7,4},{8,11},{9,10},{10,... | collective-permute-start | bytes 86024 | tf_op jit(solution)/shard_map/ppermute | solution.py:21
  3.1 5.1 %collective-permute-start.2 = (bf16[4,3584]{1,0:T(4,128)(2,1)}, bf16[4,3584]{1,0:T(4,128)(2,1)S(1)}, u32[]{:S(2)}, u32[]{:S(2)}) collective-permute-start(bf16[4,3584]{1,0:T(4,128)(2,1)} %resid_ref.1), channel_id=1, source_target_pairs={{0,7},{1,6},{2,5},{3,4},{4,3},{5,2},{6,1},{7,0},{8,15},{9,14},{10,... | collective-permute-start | bytes 86024 | tf_op jit(solution)/shard_map/ppermute | solution.py:21
  4.9 4.1 %collective-permute-start.1 = (bf16[4,3584]{1,0:T(4,128)(2,1)}, bf16[4,3584]{1,0:T(4,128)(2,1)S(1)}, u32[]{:S(2)}, u32[]{:S(2)}) collective-permute-start(bf16[4,3584]{1,0:T(4,128)(2,1)} %resid_ref.1), channel_id=1, source_target_pairs={{0,5},{1,4},{2,7},{3,6},{4,1},{5,0},{6,3},{7,2},{8,13},{9,12},{10,... | collective-permute-start | bytes 86024 | tf_op jit(solution)/shard_map/ppermute | solution.py:21
  4.9 1.4 %copy-start = (bf16[224,3584]{1,0:T(8,128)(2,1)S(1)}, bf16[224,3584]{1,0:T(8,128)(2,1)}, u32[]{:S(2)}) copy-start(bf16[224,3584]{1,0:T(8,128)(2,1)} %dec_ref.5) | copy-start | bytes 4816900
  6.3 0.7 %copy-start.3 = (bf16[4,3584]{1,0:T(4,128)(2,1)S(1)}, bf16[4,3584]{1,0:T(4,128)(2,1)}, u32[]{:S(2)}) copy-start(bf16[4,3584]{1,0:T(4,128)(2,1)} %resid_ref.1) | copy-start | bytes 86020
  7.1 0.7 %copy-start.4 = (f32[224]{0:T(256)S(1)}, f32[224]{0:T(256)}, u32[]{:S(2)}) copy-start(f32[224]{0:T(256)} %param.7) | copy-start | bytes 2692
  7.8 2.7 %copy-start.2 = (bf16[224,3584]{1,0:T(8,128)(2,1)S(1)}, bf16[224,3584]{1,0:T(8,128)(2,1)}, u32[]{:S(2)}) copy-start(bf16[224,3584]{1,0:T(8,128)(2,1)} %enc_ref.1) | copy-start | bytes 4816900
  9.1 16.3 %copy-start.5 = (f32[3584]{0:T(1024)S(1)}, f32[3584]{0:T(1024)}, u32[]{:S(2)}) copy-start(f32[3584]{0:T(1024)} %param.9) | copy-start | bytes 43012
  9.1 1.4 %collective-permute-start.3 = (bf16[4,4,3584]{2,1,0:T(4,128)(2,1)S(1)}, bf16[4,4,3584]{2,1,0:T(4,128)(2,1)S(1)}, u32[]{:S(2)}, u32[]{:S(2)}) collective-permute-start(bf16[4,4,3584]{2,1,0:T(4,128)(2,1)S(1)} %pad_maximum_fusion.1.near_ref), channel_id=1, source_target_pairs={{0,1},{1,0},{2,3},{3,2},{4,5},{5,4},{6,7},{7,6},{8,9},{9,8},{10,11... | collective-permute-start | bytes 344072 | tf_op jit(solution)/shard_map/ppermute | solution.py:21
  11.8 26.7 %copy-start.1 = (bf16[224,3584]{1,0:T(8,128)(2,1)S(1)}, bf16[224,3584]{1,0:T(8,128)(2,1)}, u32[]{:S(2)}) copy-start(bf16[224,3584]{1,0:T(8,128)(2,1)} %dec_ref.5) | copy-start | bytes 4816900
  11.8 1.6 %collective-permute-start.4 = (f32[4,4,3712]{2,1,0:T(4,128)S(1)}, f32[4,4,3712]{2,1,0:T(4,128)S(1)}, u32[]{:S(2)}, u32[]{:S(2)}) collective-permute-start(f32[4,4,3712]{2,1,0:T(4,128)S(1)} %get-tuple-element.28), channel_id=1, source_target_pairs={{0,1},{1,0},{2,3},{3,2},{4,5},{5,4},{6,7},{7,6},{8,9},{9,8},{10,11... | collective-permute-start | bytes 712712 | tf_op jit(solution)/shard_map/ppermute | solution.py:21
  13.5 4.0 %collective-permute-start.5 = (f32[4,3712]{1,0:T(4,128)S(1)}, f32[4,3712]{1,0:T(4,128)S(1)}, u32[]{:S(2)}, u32[]{:S(2)}) collective-permute-start(f32[4,3712]{1,0:T(4,128)S(1)} %get-tuple-element.37), channel_id=1, source_target_pairs={{0,3},{1,2},{2,1},{3,0},{4,7},{5,6},{6,5},{7,4},{8,11},{9,10},{10,... | collective-permute-start | bytes 178184 | tf_op jit(solution)/shard_map/ppermute | solution.py:21
  14.5 4.7 %collective-permute-start.7 = (f32[4,3712]{1,0:T(4,128)S(1)}, f32[4,3712]{1,0:T(4,128)S(1)}, u32[]{:S(2)}, u32[]{:S(2)}) collective-permute-start(f32[4,3712]{1,0:T(4,128)S(1)} %get-tuple-element.38), channel_id=1, source_target_pairs={{0,7},{1,6},{2,5},{3,4},{4,3},{5,2},{6,1},{7,0},{8,15},{9,14},{10,... | collective-permute-start | bytes 178184 | tf_op jit(solution)/shard_map/ppermute | solution.py:21
  15.7 5.1 %collective-permute-start.6 = (f32[4,3712]{1,0:T(4,128)S(1)}, f32[4,3712]{1,0:T(4,128)S(1)}, u32[]{:S(2)}, u32[]{:S(2)}) collective-permute-start(f32[4,3712]{1,0:T(4,128)S(1)} %get-tuple-element.39), channel_id=1, source_target_pairs={{0,5},{1,4},{2,7},{3,6},{4,1},{5,0},{6,3},{7,2},{8,13},{9,12},{10,... | collective-permute-start | bytes 178184 | tf_op jit(solution)/shard_map/ppermute | solution.py:21
  20.9 6.1 %collective-permute-start.10 = (f32[4,3712]{1,0:T(4,128)S(1)}, f32[4,3712]{1,0:T(4,128)S(1)}, u32[]{:S(2)}, u32[]{:S(2)}) collective-permute-start(f32[4,3712]{1,0:T(4,128)S(1)} %fusion.2.refs_0_), channel_id=1, source_target_pairs={{0,24},{8,16},{16,8},{24,0},{1,25},{9,17},{17,9},{25,1},{2,26},{10... | collective-permute-start | bytes 178184 | tf_op jit(solution)/shard_map/ppermute | solution.py:21
  24.6 5.4 %collective-permute-start.9 = (f32[4,3712]{1,0:T(4,128)S(1)}, f32[4,3712]{1,0:T(4,128)S(1)}, u32[]{:S(2)}, u32[]{:S(2)}) collective-permute-start(f32[4,3712]{1,0:T(4,128)S(1)} %fusion.2.refs_0_), channel_id=1, source_target_pairs={{0,16},{8,24},{16,0},{24,8},{1,17},{9,25},{17,1},{25,9},{2,18},{10... | collective-permute-start | bytes 178184 | tf_op jit(solution)/shard_map/ppermute | solution.py:21
  24.6 5.4 %collective-permute-start.8 = (f32[4,3712]{1,0:T(4,128)S(1)}, f32[4,3712]{1,0:T(4,128)S(1)}, u32[]{:S(2)}, u32[]{:S(2)}) collective-permute-start(f32[4,3712]{1,0:T(4,128)S(1)} %fusion.2.refs_0_), channel_id=1, source_target_pairs={{0,8},{8,0},{16,24},{24,16},{1,9},{9,1},{17,25},{25,17},{2,10},{10... | collective-permute-start | bytes 178184 | tf_op jit(solution)/shard_map/ppermute | solution.py:21
  30.7 4.9 %collective-permute-start.13 = (bf16[8,2816]{1,0:T(8,128)(2,1)S(1)}, bf16[8,2816]{1,0:T(8,128)(2,1)S(1)}, u32[]{:S(2)}, u32[]{:S(2)}) collective-permute-start(bf16[8,2816]{1,0:T(8,128)(2,1)S(1)} %get-tuple-element.30), channel_id=1, source_target_pairs={{0,7},{1,6},{2,5},{3,4},{4,3},{5,2},{6,1},{7,0},{8,15},{9,14},{10,... | collective-permute-start | bytes 135176 | tf_op jit(solution)/shard_map/ppermute | solution.py:21
  31.6 4.8 %collective-permute-start.12 = (bf16[8,2816]{1,0:T(8,128)(2,1)S(1)}, bf16[8,2816]{1,0:T(8,128)(2,1)S(1)}, u32[]{:S(2)}, u32[]{:S(2)}) collective-permute-start(bf16[8,2816]{1,0:T(8,128)(2,1)S(1)} %get-tuple-element.30), channel_id=1, source_target_pairs={{0,5},{1,4},{2,7},{3,6},{4,1},{5,0},{6,3},{7,2},{8,13},{9,12},{10,... | collective-permute-start | bytes 135176 | tf_op jit(solution)/shard_map/ppermute | solution.py:21
  33.1 3.9 %collective-permute-start.11 = (bf16[8,2816]{1,0:T(8,128)(2,1)S(1)}, bf16[8,2816]{1,0:T(8,128)(2,1)S(1)}, u32[]{:S(2)}, u32[]{:S(2)}) collective-permute-start(bf16[8,2816]{1,0:T(8,128)(2,1)S(1)} %get-tuple-element.30), channel_id=1, source_target_pairs={{0,3},{1,2},{2,1},{3,0},{4,7},{5,6},{6,5},{7,4},{8,11},{9,10},{10,... | collective-permute-start | bytes 135176 | tf_op jit(solution)/shard_map/ppermute | solution.py:21
  37.1 1.5 %collective-permute-start.14 = (bf16[4,8,2816]{2,1,0:T(8,128)(2,1)S(1)}, bf16[4,8,2816]{2,1,0:T(8,128)(2,1)S(1)}, u32[]{:S(2)}, u32[]{:S(2)}) collective-permute-start(bf16[4,8,2816]{2,1,0:T(8,128)(2,1)S(1)} %pad_maximum_fusion.near_ref), channel_id=1, source_target_pairs={{0,1},{1,0},{2,3},{3,2},{4,5},{5,4},{6,7},{7,6},{8,9},{9,8},{10,11... | collective-permute-start | bytes 540680 | tf_op jit(solution)/shard_map/ppermute | solution.py:21
where the time goes:
time: 41.1 us; the launch traced here: 40.9 us
  waiting for transfers between devices  17.4 us (42%)
  starting transfers between devices  14.9 us (36%)
  Pallas kernels  4.77 us (12%)
  local copies, waits for them, and re-layouts  2.88 us (7%)
  between operations  0.71 us (2%)
    ppermute x15, waiting for transfers between devices, swap(): return lax.ppermute(x, axis, [(i, i ^ mask) for i in range(size)])  17.4 us
    ppermute x15, starting transfers between devices, swap(): return lax.ppermute(x, axis, [(i, i ^ mask) for i in range(size)])  14.9 us
    unnamed x12, local copies, waits for them, and re-layouts  2.86 us
    pallas_call x1, Pallas kernels, per_device(): pl.pallas_call(functools.partial(backward_kernel, order), out_shape=(shap...  2.34 us
    pallas_call x1, Pallas kernels, per_device(): pl.pallas_call(forward_kernel, out_shape=(shape((half, rows, wide), F32),...  1.33 us
  transfers between devices with their start and end apart: 15, of which 12 were waited for; matrix products, arithmetic and copies ran while one was open for 0% of the time, Pallas kernels for 1%

commit v1 on v0

v1 whole, which is shorter than its diff:
```python
import functools

import jax
import jax.numpy as jnp
from jax import lax
from jax.experimental import pallas as pl
from jax.experimental.pallas import tpu as pltpu
from jax.sharding import PartitionSpec as P


epsilon = 1e-06
LANES = 128


BF16, F32 = jnp.bfloat16, jnp.float32
VMEM = pl.BlockSpec(memory_space=pltpu.VMEM)
PARAMS = pltpu.CompilerParams(vmem_limit_bytes=16 << 20)


def swap(x, axis, size, mask):
    return lax.ppermute(x, axis, [(i, i ^ mask) for i in range(size)])


def swaps(xs, axis, size, masks):
    out = []
    for x, m in zip(xs, masks):
        out.append(swap(x, axis, size, m))
    return out


def far_masks(size):
    return [0] + list(range(3, size, 2))


def tree_sum(terms):
    while len(terms) > 1:
        terms = [terms[i] + terms[i + 1] for i in range(0, len(terms), 2)]
    return terms[0]


def chunk_of(width):
    return next(c for c in (512, 384, 256, 128) if width % c == 0)


def contract(a, b, dims):
    return lax.dot_general(a, b, (dims, ((), ())), preferred_element_type=F32)


def prepare_kernel(
    dec_hbm, enc_hbm, bias_hbm, resid_hbm,
    dec_ref, enc_ref, norm_ref, bias_col_ref, own_ref, bias_buf, sems,
):
    lat, width = dec_ref.shape
    pairs = ((bias_hbm, bias_buf), (dec_hbm, dec_ref), (resid_hbm, own_ref), (enc_hbm, enc_ref))
    copies = [pltpu.make_async_copy(a, b, sems.at[k]) for k, (a, b) in enumerate(pairs)]
    for copy in copies:
        copy.start()
    copies[0].wait()
    bias_col_ref[...] = jnp.transpose(jnp.broadcast_to(bias_buf[...], (8, lat)))[:, :1]
    copies[1].wait()
    total = jnp.zeros((lat, LANES), F32)
    for c in range(0, width, LANES):
        part = dec_ref[:, c : c + LANES].astype(F32)
        total = total + part * part
    norm_ref[...] = jnp.sqrt(jnp.sum(total, axis=1, keepdims=True) + epsilon)
    copies[2].wait()
    copies[3].wait()


def decode_half(by_row, dec_ref, tail, out_ref):
    half, rows, wide = out_ref.shape
    width = wide - LANES
    for k in range(half):
        out_ref[k, :, width:] = tail
    chunk = chunk_of(width)
    for c in range(0, width, chunk):
        part = contract(by_row, dec_ref[:, c : c + chunk], ((1,), (0,)))
        for k in range(half):
            out_ref[k, :, c : c + chunk] = part[k * rows : (k + 1) * rows]


def encode_kernel(
    near_ref, other_ref, enc_ref, bias_ref, dec_ref, norm_ref,
    send_ref, near_codes_ref, tail_ref, codes_ref, scale_ref, rows_f32,
):
    half, rows, _ = near_ref.shape
    for p in range(2 * half):
        block = near_ref[p] if p < half else other_ref[p - half]
        rows_f32[p * rows : (p + 1) * rows, :] = block.astype(F32)
    stream = rows_f32[...].astype(BF16)
    preact = contract(enc_ref[...], stream, ((1,), (1,))) + bias_ref[...]
    codes = jnp.maximum(preact, 0.0).astype(BF16)
    codes_ref[...] = codes
    codes_f32 = codes.astype(F32)
    norm = norm_ref[...]
    scale_ref[...] = jnp.sum(codes_f32, axis=1, keepdims=True) / norm
    penalty = jnp.sum(codes_f32 * norm, axis=(0, 1), keepdims=True)
    tail = jnp.broadcast_to(penalty, (rows, LANES))
    tail_ref[...] = tail
    by_row = jnp.transpose(codes_f32)
    near_codes_ref[...] = by_row[: half * rows].astype(BF16)
    decode_half(by_row[half * rows :].astype(BF16), dec_ref, tail, send_ref)


def keep_kernel(near_codes_ref, tail_ref, dec_ref, keep_ref):
    decode_half(near_codes_ref[...], dec_ref, tail_ref[...], keep_ref)


def recon_of(terms, bias_ref):
    total = tree_sum([t[...] for t in terms])
    width = bias_ref.shape[1]
    return total[:, :width] + bias_ref[...], total[:1, width:]


def recon_kernel(n_terms, *refs):
    terms, (bias_ref, recon_ref) = refs[:n_terms], refs[n_terms:]
    recon_ref[...] = recon_of(terms, bias_ref)[0]


def error_kernel(n_tensor, n_terms, *refs):
    terms, (bias_ref, resid_ref, out_ref, pack) = refs[:n_terms], refs[n_terms:]
    rows, width = resid_ref.shape
    cut, piece = width // 2, width // rows
    recon, penalty = recon_of(terms, bias_ref)
    errors = recon - resid_ref[...].astype(F32)
    column = jnp.sum(errors, axis=0, keepdims=True)
    squares = jnp.zeros((rows, LANES), F32)
    for c in range(0, width, LANES):
        squares = squares + errors[:, c : c + LANES] * errors[:, c : c + LANES]
    value = 0.5 * jnp.sum(squares, axis=0, keepdims=True) + penalty * (1.0 / (n_tensor * LANES))
    pack[:rows, :cut] = errors[:, :cut]
    pack[rows:, :cut] = errors[:, cut:]
    high = column.astype(BF16).astype(F32)
    low = column - high
    for r in range(rows):
        pack[r : r + 1, cut : cut + piece] = high[:, r * piece : (r + 1) * piece]
        pack[rows + r : rows + r + 1, cut : cut + piece] = low[:, r * piece : (r + 1) * piece]
    pack[:, cut + piece :] = jnp.zeros((2 * rows, LANES), F32)
    for r in range(3):
        high = value.astype(BF16).astype(F32)
        pack[r : r + 1, cut + piece :] = high
        value = value - high
    out_ref[...] = pack[...].astype(BF16)


def backward_kernel(
    order, near_ref, other_ref, codes_ref, scale_ref, dec_ref, norm_ref,
    grad_ref, code_grad_ref, column_ref, loss_ref,
    errors_ref, staged, by_row_ref, column_buf, loss_buf, sems, small_sems,
):
    half, rows2, _ = near_ref.shape
    rows = rows2 // 2
    _, width = dec_ref.shape
    cut, piece = width // 2, width // rows
    blocks = [near_ref.at[p] if p < half else other_ref.at[p - half] for p in range(2 * half)]
    codes, scale = codes_ref[...], scale_ref[...]
    chunk = staged.shape[2]
    copies = []

    def write(source, target, sem):
        copies.append(pltpu.make_async_copy(source, target, sem))
        copies[-1].start()

    for i in range(width // chunk):
        cols = slice(i * chunk, (i + 1) * chunk)
        low = i * chunk % cut
        first = rows * (i * chunk // cut)
        part = [b[:, low : low + chunk].astype(F32)[first : first + rows] for b in blocks]
        errors = jnp.concatenate(part).astype(BF16)
        errors_ref[:, cols] = errors
        grad = contract(codes, errors, ((1,), (0,)))
        staged[i] = (grad + scale * dec_ref[:, cols].astype(F32)).astype(BF16)
        write(staged.at[i], grad_ref.at[:, cols], sems.at[i])

    by_lat = contract(dec_ref[...], errors_ref[...], ((1,), (1,))) + norm_ref[...]
    by_row = jnp.transpose(by_lat)
    me = lax.axis_index("tensor")
    for p, mask in enumerate(order[:half]):
        block = lax.bitwise_xor(me, mask)
        one = by_row[p * rows : (p + 1) * rows]
        two = by_row[(half + p) * rows : (half + p + 1) * rows]
        if len(by_row_ref.shape) == 3:
            by_row_ref[block] = one
            by_row_ref[lax.bitwise_xor(block, 1)] = two
        else:
            odd = lax.rem(block, 2) == 1
            both = jnp.concatenate([jnp.where(odd, two, one), jnp.where(odd, one, two)])
            start = pl.multiple_of(lax.div(block, 2) * 2 * rows, 2 * rows)
            by_row_ref[pl.ds(start, 2 * rows), :] = both
    write(by_row_ref, code_grad_ref, small_sems.at[0])

    columns, losses = {}, {}
    for p, mask in enumerate(order):
        ends = blocks[p][:, cut:].astype(F32)
        columns[mask] = ends[:rows, :piece] + ends[rows:, :piece]
        losses[mask] = (ends[0:1, piece:] + ends[1:2, piece:]) + ends[2:3, piece:]
    column = tree_sum([columns[m] for m in range(len(order))])
    for r in range(rows):
        column_buf[r * piece : (r + 1) * piece] = column[r]
    write(column_buf, column_ref, small_sems.at[1])
    loss = tree_sum([losses[m] for m in range(len(order))])
    loss_buf[...] = jnp.sum(loss, axis=1, keepdims=True) / (len(order) * rows * width)
    write(loss_buf, loss_ref, small_sems.at[2])
    for copy in copies:
        copy.wait()


def per_device(n_section, n_tensor, resid, w_enc, b_enc, w_dec, b_dec):
    rows, width = resid.shape
    lat = w_enc.shape[0]
    masks = far_masks(n_tensor)
    order = masks + [m ^ 1 for m in masks]
    half = len(masks)
    total_rows = n_tensor * rows
    wide = width + LANES
    shape = jax.ShapeDtypeStruct

    anywhere = pl.BlockSpec(memory_space=pl.ANY)
    stored = [
        pltpu.with_memory_space_constraint(x, pltpu.HBM)
        for x in (w_dec, w_enc, b_enc.reshape(1, lat), resid)
    ]
    w_dec, w_enc, norm, bias, own = pl.pallas_call(
        prepare_kernel,
        out_shape=(
            shape((lat, width), BF16),
            shape((lat, width), BF16),
            shape((lat, 1), F32),
            shape((lat, 1), F32),
            shape((rows, width), BF16),
        ),
        in_specs=[anywhere] * 4,
        out_specs=(VMEM,) * 5,
        compiler_params=PARAMS,
        scratch_shapes=[pltpu.VMEM((1, lat), F32), pltpu.SemaphoreType.DMA((4,))],
    )(*stored)
    near = jnp.stack([own] + swaps([resid] * half, "tensor", n_tensor, masks[1:]))
    near, norm = lax.optimization_barrier((near, norm))
    other = swap(near, "tensor", n_tensor, 1)
    send, near_codes, tail, codes, scale = pl.pallas_call(
        encode_kernel,
        out_shape=(
            shape((half, rows, wide), F32),
            shape((half * rows, lat), BF16),
            shape((rows, LANES), F32),
            shape((lat, total_rows), BF16),
            shape((lat, 1), F32),
        ),
        in_specs=[VMEM] * 6,
        out_specs=(VMEM,) * 5,
        compiler_params=PARAMS,
        scratch_shapes=[pltpu.VMEM((total_rows, width), F32)],
    )(near, other, w_enc, bias, w_dec, norm)
    (received,) = swaps([send], "tensor", n_tensor, [1])
    keep = pl.pallas_call(
        keep_kernel,
        out_shape=shape((half, rows, wide), F32),
        in_specs=[VMEM] * 3,
        out_specs=VMEM,
        compiler_params=PARAMS,
    )(near_codes, tail, w_dec)
    pair = keep + received
    share = pair[0]
    for part in swaps(list(pair[1:]), "tensor", n_tensor, masks[1:]):
        share = share + part
    across = range(1, n_section)
    terms = [share] + swaps([share] * n_section, "section", n_section, across)
    packed = width // 2 + width // rows + LANES
    bias = b_dec.reshape(1, width)
    payload = pl.pallas_call(
        functools.partial(error_kernel, n_tensor, len(terms)),
        out_shape=shape((2 * rows, packed), BF16),
        in_specs=[VMEM] * (len(terms) + 2),
        out_specs=VMEM,
        compiler_params=PARAMS,
        scratch_shapes=[pltpu.VMEM((2 * rows, packed), F32)],
    )(*terms, bias, own)
    near = jnp.stack([payload] + swaps([payload] * half, "tensor", n_tensor, masks[1:]))
    recon = pl.pallas_call(
        functools.partial(recon_kernel, len(terms)),
        out_shape=shape((rows, width), F32),
        in_specs=[VMEM] * (len(terms) + 1),
        out_specs=VMEM,
        compiler_params=PARAMS,
    )(*terms, bias)
    other = swap(near, "tensor", n_tensor, 1)
    chunk = chunk_of(width // 2)
    n_chunks = width // chunk
    by_row = (total_rows, lat) if rows % 4 == 0 else (n_tensor, rows, lat)
    grad_w_dec, code_grad, column, loss = pl.pallas_call(
        functools.partial(backward_kernel, order),
        out_shape=(
            shape((lat, width), BF16),
            shape(by_row, F32),
            shape((width,), F32),
            shape((1, 1), F32),
        ),
        in_specs=[VMEM] * 6,
        out_specs=(anywhere,) * 4,
        compiler_params=PARAMS,
        scratch_shapes=[
            pltpu.VMEM((total_rows, width), BF16),
            pltpu.VMEM((n_chunks, lat, chunk), BF16),
            pltpu.VMEM(by_row, F32),
            pltpu.VMEM((width,), F32),
            pltpu.VMEM((1, 1), F32),
            pltpu.SemaphoreType.DMA((n_chunks,)),
            pltpu.SemaphoreType.DMA((3,)),
        ],
    )(near, other, codes, scale, w_dec, norm)
    return recon, grad_w_dec, code_grad.reshape(total_rows, lat), column, loss.reshape(())


def solution(mesh):
    n_section, n_tensor = mesh.shape["section"], mesh.shape["tensor"]
    in_specs = (
        P("tensor", None),
        P(("section", "tensor"), None),
        P(("section", "tensor")),
        P(("section", "tensor"), None),
        P(),
    )
    out_specs = (
        P("tensor", None),
        P(("section", "tensor"), None),
        P(None, ("section", "tensor")),
        P(),
        P(),
    )

    def body(*args):
        return per_device(n_section, n_tensor, *args)

    return jax.shard_map(body, mesh=mesh, in_specs=in_specs, out_specs=out_specs, check_vma=False)
```

time: 41.1 us -> 39.2 us (0.954)
  local copies, waits for them, and re-layouts: 2.88 us -> 0.03 us
  Pallas kernels: 4.77 us -> 6.18 us
    unnamed x12 -> x2, local copies, waits for them, and re-layouts: 2.86 us -> 0.01 us
    pallas_call x2 -> x4, Pallas kernels: 1.76 us -> 4.25 us  [the longest x1 1.97 us: per_device(): pl.pallas_call(prepare_kernel, out_shape=(shape((lat, width), BF16), shap...]
    pallas_call x1, Pallas kernels: 0.67 us -> 0.11 us  [per_device(): pl.pallas_call(functools.partial(error_kernel, n_tensor, len(terms)), out...]
    pallas_call x1, Pallas kernels: 2.34 us -> 1.82 us  [per_device(): pl.pallas_call(functools.partial(backward_kernel, order), out_shape=(shap...]
  transfers between devices with their start and end apart: 15 -> 15, of which waited for: 12 -> 12; matrix products, arithmetic and copies ran while one was open for 0% -> 0% of each run, Pallas kernels for 1% -> 8%
where the time goes in v1:
time: 39.2 us; the launch traced here: 39 us
  waiting for transfers between devices  17.3 us (44%)
  starting transfers between devices  14.5 us (37%)
  Pallas kernels  6.18 us (16%)
  between operations  0.7 us (2%)
    ppermute x15, waiting for transfers between devices, swap(): return lax.ppermute(x, axis, [(i, i ^ mask) for i in range(size)])  17.3 us
    ppermute x15, starting transfers between devices, swap(): return lax.ppermute(x, axis, [(i, i ^ mask) for i in range(size)])  14.5 us
    pallas_call x1, Pallas kernels, per_device(): pl.pallas_call(prepare_kernel, out_shape=(shape((lat, width), BF16), shap...  1.97 us
    pallas_call x1, Pallas kernels, per_device(): pl.pallas_call(functools.partial(backward_kernel, order), out_shape=(shap...  1.82 us
    pallas_call x1, Pallas kernels, per_device(): pl.pallas_call(encode_kernel, out_shape=(shape((half, rows, wide), F32),...  1.32 us
  transfers between devices with their start and end apart: 15, of which 12 were waited for; matrix products, arithmetic and copies ran while one was open for 0% of the time, Pallas kernels for 8%

profile of v1, /device:TPU:0, one launch (start us, length us, event | category | flops | bytes accessed | tf_op | source)
XLA Modules:
  0.0 39.0 jit_solution(13246561211734193814)
XLA Ops:
  0.6 3.4 %collective-permute-start.2 = (bf16[4,3584]{1,0:T(4,128)(2,1)}, bf16[4,3584]{1,0:T(4,128)(2,1)S(1)}, u32[]{:S(2)}, u32[]{:S(2)}) collective-permute-start(bf16[4,3584]{1,0:T(4,128)(2,1)} %resid_hbm.1), channel_id=1, source_target_pairs={{0,7},{1,6},{2,5},{3,4},{4,3},{5,2},{6,1},{7,0},{8,15},{9,14},{10,... | collective-permute-start | bytes 86024 | tf_op jit(solution)/shard_map/ppermute | solution.py:21
  4.1 0.8 %collective-permute-start.1 = (bf16[4,3584]{1,0:T(4,128)(2,1)}, bf16[4,3584]{1,0:T(4,128)(2,1)S(1)}, u32[]{:S(2)}, u32[]{:S(2)}) collective-permute-start(bf16[4,3584]{1,0:T(4,128)(2,1)} %resid_hbm.1), channel_id=1, source_target_pairs={{0,5},{1,4},{2,7},{3,6},{4,1},{5,0},{6,3},{7,2},{8,13},{9,12},{10,... | collective-permute-start | bytes 86024 | tf_op jit(solution)/shard_map/ppermute | solution.py:21
  4.8 0.1 collective-permute-start
  5.0 2.0 %shard_map.92 = (bf16[224,3584]{1,0:T(8,128)(2,1)S(1)}, bf16[224,3584]{1,0:T(8,128)(2,1)S(1)}, f32[224,1]{1,0:T(8,128)S(1)}, f32[224,1]{1,0:T(8,128)S(1)}, bf16[4,3584]{1,0:T(4,128)(2,1)S(1)}) custom-call(bf16[224,3584]{1,0:T(8,128)(2,1)} %dec_hbm.1, bf16[224,3584]{1,0:T(8,128)(2,1)} %enc_hbm.1, f32[1,224]{1,0:T(1,128)} %bitcast.32, bf16[4,3584]{1,0:T(4,128)(2,1)} %resid_hbm.1), custom_call_target="tpu_custom_call" | custom-call | tf_op jit(solution)/shard_map/pallas_call | solution.py:223
  7.0 0.0 collective-permute-done.2
  7.0 0.6 %collective-permute-done.1 = bf16[4,3584]{1,0:T(4,128)(2,1)S(1)} collective-permute-done((bf16[4,3584]{1,0:T(4,128)(2,1)}, bf16[4,3584]{1,0:T(4,128)(2,1)S(1)}, u32[]{:S(2)}, u32[]{:S(2)}) %collective-permute-start.1) | collective-permute-done | bytes 28704 | tf_op jit(solution)/shard_map/ppermute | solution.py:21
  7.6 1.0 %collective-permute-done = bf16[4,3584]{1,0:T(4,128)(2,1)S(1)} collective-permute-done((bf16[4,3584]{1,0:T(4,128)(2,1)}, bf16[4,3584]{1,0:T(4,128)(2,1)S(1)}, u32[]{:S(2)}, u32[]{:S(2)}) %collective-permute-start) | collective-permute-done | bytes 28704 | tf_op jit(solution)/shard_map/ppermute | solution.py:21
  8.6 0.1 pad_maximum_fusion.1.near_ref
  8.7 0.2 collective-permute-start.3
  8.9 1.2 %collective-permute-done.3.other_ref = bf16[4,4,3584]{2,1,0:T(4,128)(2,1)S(1)} collective-permute-done((bf16[4,4,3584]{2,1,0:T(4,128)(2,1)S(1)}, bf16[4,4,3584]{2,1,0:T(4,128)(2,1)S(1)}, u32[]{:S(2)}, u32[]{:S(2)}) %collective-permute-start.3) | collective-permute-done | bytes 114720 | tf_op jit(solution)/shard_map/ppermute | solution.py:21
  10.1 1.3 %shard_map.93 = (f32[4,4,3712]{2,1,0:T(4,128)S(1)}, bf16[16,224]{1,0:T(8,128)(2,1)S(1)}, f32[4,128]{1,0:T(4,128)S(1)}, bf16[224,32]{1,0:T(8,128)(2,1)S(1)}, f32[224,1]{1,0:T(8,128)S(1)}) custom-call(bf16[4,4,3584]{2,1,0:T(4,128)(2,1)S(1)} %pad_maximum_fusion.1.near_ref, bf16[4,4,3584]{2,1,0:T(4,128)(2,1)S(1)} %collective-permute-done.3.other_ref, ...), custom_call_target="tpu_custom_call" | custom-call | tf_op jit(solution)/shard_map/pallas_call | solution.py:240
  11.4 0.2 collective-permute-start.4
  11.6 0.0 copy-start
  11.6 0.3 shard_map.94
  11.9 1.0 %collective-permute-done.4 = f32[4,4,3712]{2,1,0:T(4,128)S(1)} collective-permute-done((f32[4,4,3712]{2,1,0:T(4,128)S(1)}, f32[4,4,3712]{2,1,0:T(4,128)S(1)}, u32[]{:S(2)}, u32[]{:S(2)}) %collective-permute-start.4) | collective-permute-done | bytes 237600 | tf_op jit(solution)/shard_map/ppermute | solution.py:21
  12.9 0.1 add.12
  13.0 1.3 %collective-permute-start.7 = (f32[4,3712]{1,0:T(4,128)S(1)}, f32[4,3712]{1,0:T(4,128)S(1)}, u32[]{:S(2)}, u32[]{:S(2)}) collective-permute-start(f32[4,3712]{1,0:T(4,128)S(1)} %get-tuple-element.38), channel_id=1, source_target_pairs={{0,7},{1,6},{2,5},{3,4},{4,3},{5,2},{6,1},{7,0},{8,15},{9,14},{10,... | collective-permute-start | bytes 178184 | tf_op jit(solution)/shard_map/ppermute | solution.py:21
  14.3 0.2 collective-permute-start.6
  14.5 1.6 %collective-permute-start.5 = (f32[4,3712]{1,0:T(4,128)S(1)}, f32[4,3712]{1,0:T(4,128)S(1)}, u32[]{:S(2)}, u32[]{:S(2)}) collective-permute-start(f32[4,3712]{1,0:T(4,128)S(1)} %get-tuple-element.37), channel_id=1, source_target_pairs={{0,3},{1,2},{2,1},{3,0},{4,7},{5,6},{6,5},{7,4},{8,11},{9,10},{10,... | collective-permute-start | bytes 178184 | tf_op jit(solution)/shard_map/ppermute | solution.py:21
  16.1 1.9 %collective-permute-done.7 = f32[4,3712]{1,0:T(4,128)S(1)} collective-permute-done((f32[4,3712]{1,0:T(4,128)S(1)}, f32[4,3712]{1,0:T(4,128)S(1)}, u32[]{:S(2)}, u32[]{:S(2)}) %collective-permute-start.7) | collective-permute-done | bytes 59424 | tf_op jit(solution)/shard_map/ppermute | solution.py:21
  18.0 1.5 %collective-permute-done.6 = f32[4,3712]{1,0:T(4,128)S(1)} collective-permute-done((f32[4,3712]{1,0:T(4,128)S(1)}, f32[4,3712]{1,0:T(4,128)S(1)}, u32[]{:S(2)}, u32[]{:S(2)}) %collective-permute-start.6) | collective-permute-done | bytes 59424 | tf_op jit(solution)/shard_map/ppermute | solution.py:21
  19.5 0.0 collective-permute-done.5
  19.5 1.6 %collective-permute-start.8 = (f32[4,3712]{1,0:T(4,128)S(1)}, f32[4,3712]{1,0:T(4,128)S(1)}, u32[]{:S(2)}, u32[]{:S(2)}) collective-permute-start(f32[4,3712]{1,0:T(4,128)S(1)} %fusion.2.refs_0_), channel_id=1, source_target_pairs={{0,8},{8,0},{16,24},{24,16},{1,9},{9,1},{17,25},{25,17},{2,10},{10... | collective-permute-start | bytes 178184 | tf_op jit(solution)/shard_map/ppermute | solution.py:21
  21.1 2.6 %collective-permute-start.9 = (f32[4,3712]{1,0:T(4,128)S(1)}, f32[4,3712]{1,0:T(4,128)S(1)}, u32[]{:S(2)}, u32[]{:S(2)}) collective-permute-start(f32[4,3712]{1,0:T(4,128)S(1)} %fusion.2.refs_0_), channel_id=1, source_target_pairs={{0,16},{8,24},{16,0},{24,8},{1,17},{9,25},{17,1},{25,9},{2,18},{10... | collective-permute-start | bytes 178184 | tf_op jit(solution)/shard_map/ppermute | solution.py:21
  23.7 0.2 collective-permute-start.10
  24.0 0.0 copy-done
  24.0 0.0 collective-permute-done.8.refs_1_
  24.0 3.6 %collective-permute-done.9.refs_2_ = f32[4,3712]{1,0:T(4,128)S(1)} collective-permute-done((f32[4,3712]{1,0:T(4,128)S(1)}, f32[4,3712]{1,0:T(4,128)S(1)}, u32[]{:S(2)}, u32[]{:S(2)}) %collective-permute-start.9) | collective-permute-done | bytes 59424 | tf_op jit(solution)/shard_map/ppermute | solution.py:21
  27.6 2.1 %collective-permute-done.10.refs_3_ = f32[4,3712]{1,0:T(4,128)S(1)} collective-permute-done((f32[4,3712]{1,0:T(4,128)S(1)}, f32[4,3712]{1,0:T(4,128)S(1)}, u32[]{:S(2)}, u32[]{:S(2)}) %collective-permute-start.10) | collective-permute-done | bytes 59424 | tf_op jit(solution)/shard_map/ppermute | solution.py:21
  29.7 0.1 shard_map.96
  29.8 0.1 collective-permute-start.13
  29.9 1.9 %collective-permute-start.12 = (bf16[8,2816]{1,0:T(8,128)(2,1)S(1)}, bf16[8,2816]{1,0:T(8,128)(2,1)S(1)}, u32[]{:S(2)}, u32[]{:S(2)}) collective-permute-start(bf16[8,2816]{1,0:T(8,128)(2,1)S(1)} %shard_map.96), channel_id=1, source_target_pairs={{0,5},{1,4},{2,7},{3,6},{4,1},{5,0},{6,3},{7,2},{8,13},{9,12},{10,... | collective-permute-start | bytes 135176 | tf_op jit(solution)/shard_map/ppermute | solution.py:21
  31.8 0.2 collective-permute-start.11
  32.0 2.2 %collective-permute-done.13 = bf16[8,2816]{1,0:T(8,128)(2,1)S(1)} collective-permute-done((bf16[8,2816]{1,0:T(8,128)(2,1)S(1)}, bf16[8,2816]{1,0:T(8,128)(2,1)S(1)}, u32[]{:S(2)}, u32[]{:S(2)}) %collective-permute-start.13) | collective-permute-done | bytes 45088 | tf_op jit(solution)/shard_map/ppermute | solution.py:21
  34.3 0.3 collective-permute-done.12
  34.5 1.1 %collective-permute-done.11 = bf16[8,2816]{1,0:T(8,128)(2,1)S(1)} collective-permute-done((bf16[8,2816]{1,0:T(8,128)(2,1)S(1)}, bf16[8,2816]{1,0:T(8,128)(2,1)S(1)}, u32[]{:S(2)}, u32[]{:S(2)}) %collective-permute-start.11) | collective-permute-done | bytes 45088 | tf_op jit(solution)/shard_map/ppermute | solution.py:21
  35.7 0.2 collective-permute-start.14
  35.9 0.6 %shard_map.95 = f32[4,3584]{1,0:T(4,128)} custom-call(f32[4,3712]{1,0:T(4,128)S(1)} %fusion.2.refs_0_, f32[4,3712]{1,0:T(4,128)S(1)} %collective-permute-done.8.refs_1_, f32[4,3712]{1,0:T(4,128)S(1)} %collective-permute-done.9.refs_2_, f32[4,3712]{1,0:T(4,128)S(1)} %collective-permute-done.10.refs_3_, f32[1,3584]{1,0:T(1,128)S(1)} %reshape.20.refs_4_), custom_call_target="tpu_custom_call" | custom-call | tf_op jit(solution)/shard_map/pallas_call | solution.py:279
  36.5 0.7 %collective-permute-done.14.other_ref = bf16[4,8,2816]{2,1,0:T(8,128)(2,1)S(1)} collective-permute-done((bf16[4,8,2816]{2,1,0:T(8,128)(2,1)S(1)}, bf16[4,8,2816]{2,1,0:T(8,128)(2,1)S(1)}, u32[]{:S(2)}, u32[]{:S(2)}) %collective-permute-start.14) | collective-permute-done | bytes 180256 | tf_op jit(solution)/shard_map/ppermute | solution.py:21
  37.2 1.8 %shard_map.97 = (bf16[224,3584]{1,0:T(8,128)(2,1)}, f32[32,224]{1,0:T(8,128)}, f32[3584]{0:T(1024)}, f32[1,1]{1,0:T(1,128)}) custom-call(bf16[4,8,2816]{2,1,0:T(8,128)(2,1)S(1)} %pad_maximum_fusion.near_ref, bf16[4,8,2816]{2,1,0:T(8,128)(2,1)S(1)} %collective-permute-done.14.other_ref, bf16[224,32]{1,0:T(8,128)(2,1)S(1)} %get-tuple-element.31.codes_ref, ...), custom_call_target="tpu_custom_call" | custom-call | tf_op jit(solution)/shard_map/pallas_call | solution.py:290
  (4 shorter events, 0.1 us)
Async XLA Ops:
  0.6 6.3 %collective-permute-start.2 = (bf16[4,3584]{1,0:T(4,128)(2,1)}, bf16[4,3584]{1,0:T(4,128)(2,1)S(1)}, u32[]{:S(2)}, u32[]{:S(2)}) collective-permute-start(bf16[4,3584]{1,0:T(4,128)(2,1)} %resid_hbm.1), channel_id=1, source_target_pairs={{0,7},{1,6},{2,5},{3,4},{4,3},{5,2},{6,1},{7,0},{8,15},{9,14},{10,... | collective-permute-start | bytes 86024 | tf_op jit(solution)/shard_map/ppermute | solution.py:21
  4.1 3.5 %collective-permute-start.1 = (bf16[4,3584]{1,0:T(4,128)(2,1)}, bf16[4,3584]{1,0:T(4,128)(2,1)S(1)}, u32[]{:S(2)}, u32[]{:S(2)}) collective-permute-start(bf16[4,3584]{1,0:T(4,128)(2,1)} %resid_hbm.1), channel_id=1, source_target_pairs={{0,5},{1,4},{2,7},{3,6},{4,1},{5,0},{6,3},{7,2},{8,13},{9,12},{10,... | collective-permute-start | bytes 86024 | tf_op jit(solution)/shard_map/ppermute | solution.py:21
  4.8 3.7 %collective-permute-start = (bf16[4,3584]{1,0:T(4,128)(2,1)}, bf16[4,3584]{1,0:T(4,128)(2,1)S(1)}, u32[]{:S(2)}, u32[]{:S(2)}) collective-permute-start(bf16[4,3584]{1,0:T(4,128)(2,1)} %resid_hbm.1), channel_id=1, source_target_pairs={{0,3},{1,2},{2,1},{3,0},{4,7},{5,6},{6,5},{7,4},{8,11},{9,10},{10,... | collective-permute-start | bytes 86024 | tf_op jit(solution)/shard_map/ppermute | solution.py:21
  8.7 1.4 %collective-permute-start.3 = (bf16[4,4,3584]{2,1,0:T(4,128)(2,1)S(1)}, bf16[4,4,3584]{2,1,0:T(4,128)(2,1)S(1)}, u32[]{:S(2)}, u32[]{:S(2)}) collective-permute-start(bf16[4,4,3584]{2,1,0:T(4,128)(2,1)S(1)} %pad_maximum_fusion.1.near_ref), channel_id=1, source_target_pairs={{0,1},{1,0},{2,3},{3,2},{4,5},{5,4},{6,7},{7,6},{8,9},{9,8},{10,11... | collective-permute-start | bytes 344072 | tf_op jit(solution)/shard_map/ppermute | solution.py:21
  11.4 1.5 %collective-permute-start.4 = (f32[4,4,3712]{2,1,0:T(4,128)S(1)}, f32[4,4,3712]{2,1,0:T(4,128)S(1)}, u32[]{:S(2)}, u32[]{:S(2)}) collective-permute-start(f32[4,4,3712]{2,1,0:T(4,128)S(1)} %get-tuple-element.30), channel_id=1, source_target_pairs={{0,1},{1,0},{2,3},{3,2},{4,5},{5,4},{6,7},{7,6},{8,9},{9,8},{10,11... | collective-permute-start | bytes 712712 | tf_op jit(solution)/shard_map/ppermute | solution.py:21
  11.6 12.4 %copy-start = (f32[3584]{0:T(1024)S(1)}, f32[3584]{0:T(1024)}, u32[]{:S(2)}) copy-start(f32[3584]{0:T(1024)} %param.9) | copy-start | bytes 43012
  13.0 5.0 %collective-permute-start.7 = (f32[4,3712]{1,0:T(4,128)S(1)}, f32[4,3712]{1,0:T(4,128)S(1)}, u32[]{:S(2)}, u32[]{:S(2)}) collective-permute-start(f32[4,3712]{1,0:T(4,128)S(1)} %get-tuple-element.38), channel_id=1, source_target_pairs={{0,7},{1,6},{2,5},{3,4},{4,3},{5,2},{6,1},{7,0},{8,15},{9,14},{10,... | collective-permute-start | bytes 178184 | tf_op jit(solution)/shard_map/ppermute | solution.py:21
  14.3 5.1 %collective-permute-start.6 = (f32[4,3712]{1,0:T(4,128)S(1)}, f32[4,3712]{1,0:T(4,128)S(1)}, u32[]{:S(2)}, u32[]{:S(2)}) collective-permute-start(f32[4,3712]{1,0:T(4,128)S(1)} %get-tuple-element.39), channel_id=1, source_target_pairs={{0,5},{1,4},{2,7},{3,6},{4,1},{5,0},{6,3},{7,2},{8,13},{9,12},{10,... | collective-permute-start | bytes 178184 | tf_op jit(solution)/shard_map/ppermute | solution.py:21
  14.5 5.0 %collective-permute-start.5 = (f32[4,3712]{1,0:T(4,128)S(1)}, f32[4,3712]{1,0:T(4,128)S(1)}, u32[]{:S(2)}, u32[]{:S(2)}) collective-permute-start(f32[4,3712]{1,0:T(4,128)S(1)} %get-tuple-element.37), channel_id=1, source_target_pairs={{0,3},{1,2},{2,1},{3,0},{4,7},{5,6},{6,5},{7,4},{8,11},{9,10},{10,... | collective-permute-start | bytes 178184 | tf_op jit(solution)/shard_map/ppermute | solution.py:21
  19.5 4.5 %collective-permute-start.8 = (f32[4,3712]{1,0:T(4,128)S(1)}, f32[4,3712]{1,0:T(4,128)S(1)}, u32[]{:S(2)}, u32[]{:S(2)}) collective-permute-start(f32[4,3712]{1,0:T(4,128)S(1)} %fusion.2.refs_0_), channel_id=1, source_target_pairs={{0,8},{8,0},{16,24},{24,16},{1,9},{9,1},{17,25},{25,17},{2,10},{10... | collective-permute-start | bytes 178184 | tf_op jit(solution)/shard_map/ppermute | solution.py:21
  21.1 6.5 %collective-permute-start.9 = (f32[4,3712]{1,0:T(4,128)S(1)}, f32[4,3712]{1,0:T(4,128)S(1)}, u32[]{:S(2)}, u32[]{:S(2)}) collective-permute-start(f32[4,3712]{1,0:T(4,128)S(1)} %fusion.2.refs_0_), channel_id=1, source_target_pairs={{0,16},{8,24},{16,0},{24,8},{1,17},{9,25},{17,1},{25,9},{2,18},{10... | collective-permute-start | bytes 178184 | tf_op jit(solution)/shard_map/ppermute | solution.py:21
  23.7 6.0 %collective-permute-start.10 = (f32[4,3712]{1,0:T(4,128)S(1)}, f32[4,3712]{1,0:T(4,128)S(1)}, u32[]{:S(2)}, u32[]{:S(2)}) collective-permute-start(f32[4,3712]{1,0:T(4,128)S(1)} %fusion.2.refs_0_), channel_id=1, source_target_pairs={{0,24},{8,16},{16,8},{24,0},{1,25},{9,17},{17,9},{25,1},{2,26},{10... | collective-permute-start | bytes 178184 | tf_op jit(solution)/shard_map/ppermute | solution.py:21
  29.8 4.4 %collective-permute-start.13 = (bf16[8,2816]{1,0:T(8,128)(2,1)S(1)}, bf16[8,2816]{1,0:T(8,128)(2,1)S(1)}, u32[]{:S(2)}, u32[]{:S(2)}) collective-permute-start(bf16[8,2816]{1,0:T(8,128)(2,1)S(1)} %shard_map.96), channel_id=1, source_target_pairs={{0,7},{1,6},{2,5},{3,4},{4,3},{5,2},{6,1},{7,0},{8,15},{9,14},{10,... | collective-permute-start | bytes 135176 | tf_op jit(solution)/shard_map/ppermute | solution.py:21
  29.9 4.6 %collective-permute-start.12 = (bf16[8,2816]{1,0:T(8,128)(2,1)S(1)}, bf16[8,2816]{1,0:T(8,128)(2,1)S(1)}, u32[]{:S(2)}, u32[]{:S(2)}) collective-permute-start(bf16[8,2816]{1,0:T(8,128)(2,1)S(1)} %shard_map.96), channel_id=1, source_target_pairs={{0,5},{1,4},{2,7},{3,6},{4,1},{5,0},{6,3},{7,2},{8,13},{9,12},{10,... | collective-permute-start | bytes 135176 | tf_op jit(solution)/shard_map/ppermute | solution.py:21
  31.8 3.8 %collective-permute-start.11 = (bf16[8,2816]{1,0:T(8,128)(2,1)S(1)}, bf16[8,2816]{1,0:T(8,128)(2,1)S(1)}, u32[]{:S(2)}, u32[]{:S(2)}) collective-permute-start(bf16[8,2816]{1,0:T(8,128)(2,1)S(1)} %shard_map.96), channel_id=1, source_target_pairs={{0,3},{1,2},{2,1},{3,0},{4,7},{5,6},{6,5},{7,4},{8,11},{9,10},{10,... | collective-permute-start | bytes 135176 | tf_op jit(solution)/shard_map/ppermute | solution.py:21
  35.7 1.5 %collective-permute-start.14 = (bf16[4,8,2816]{2,1,0:T(8,128)(2,1)S(1)}, bf16[4,8,2816]{2,1,0:T(8,128)(2,1)S(1)}, u32[]{:S(2)}, u32[]{:S(2)}) collective-permute-start(bf16[4,8,2816]{2,1,0:T(8,128)(2,1)S(1)} %pad_maximum_fusion.near_ref), channel_id=1, source_target_pairs={{0,1},{1,0},{2,3},{3,2},{4,5},{5,4},{6,7},{7,6},{8,9},{9,8},{10,11... | collective-permute-start | bytes 540680 | tf_op jit(solution)/shard_map/ppermute | solution.py:21

commit v2 on v1

v2 whole, which is shorter than its diff:
```python
import functools

import jax
import jax.numpy as jnp
from jax import lax
from jax.experimental import pallas as pl
from jax.experimental.pallas import tpu as pltpu
from jax.sharding import PartitionSpec as P


epsilon = 1e-06
LANES = 128


BF16, F32 = jnp.bfloat16, jnp.float32
VMEM = pl.BlockSpec(memory_space=pltpu.VMEM)
PARAMS = pltpu.CompilerParams(vmem_limit_bytes=16 << 20)


def swap(x, axis, size, mask):
    return lax.ppermute(x, axis, [(i, i ^ mask) for i in range(size)])


def swaps(xs, axis, size, masks):
    out = []
    for x, m in zip(xs, masks):
        out.append(swap(x, axis, size, m))
    return out


def far_masks(size):
    return [0] + list(range(3, size, 2))


def tree_sum(terms):
    while len(terms) > 1:
        terms = [terms[i] + terms[i + 1] for i in range(0, len(terms), 2)]
    return terms[0]


def chunk_of(width):
    return next(c for c in (512, 384, 256, 128) if width % c == 0)


def contract(a, b, dims):
    return lax.dot_general(a, b, (dims, ((), ())), preferred_element_type=F32)


def fetch_kernel(dec_hbm, enc_hbm, bias_hbm, resid_hbm, dec_ref, enc_ref, bias_ref, own_ref, sems):
    pairs = ((enc_hbm, enc_ref), (dec_hbm, dec_ref), (bias_hbm, bias_ref), (resid_hbm, own_ref))
    copies = [pltpu.make_async_copy(a, b, sems.at[k]) for k, (a, b) in enumerate(pairs)]
    for copy in copies:
        copy.start()
    for copy in copies:
        copy.wait()


def forward_kernel(half, *refs):
    blocks, refs = refs[:half], refs[half:]
    encs, biases, dec_ref = refs[0:2], refs[2:4], refs[4]
    part_ref, codes_refs = refs[5], refs[6:]
    rows, width = blocks[0].shape
    lat = encs[0].shape[0]
    chunk = chunk_of(width)
    by_lat = [jnp.zeros((lat, half * rows), F32) for _ in encs]
    for c in range(0, width, chunk):
        stream = jnp.concatenate([b[:, c : c + chunk].astype(F32) for b in blocks]).astype(BF16)
        for k, enc in enumerate(encs):
            by_lat[k] = by_lat[k] + contract(enc[:, c : c + chunk], stream, ((1,), (1,)))
    for k, codes_ref in enumerate(codes_refs):
        preact = jnp.transpose(by_lat[k]) + biases[k][...]
        codes_ref[...] = jnp.maximum(preact, 0.0).astype(BF16)
    for c in range(0, width, chunk):
        cols = slice(c, c + chunk)
        part_ref[:, cols] = contract(codes_refs[0][...], dec_ref[:, cols], ((1,), (0,)))


def mate_kernel(part_ref, codes_ref, dec_ref, *shares):
    rows, width = shares[0].shape
    chunk = chunk_of(width)
    for c in range(0, width, chunk):
        cols = slice(c, c + chunk)
        total = part_ref[:, cols] + contract(codes_ref[...], dec_ref[:, cols], ((1,), (0,)))
        for k, share in enumerate(shares):
            share[:, cols] = total[k * rows : (k + 1) * rows]


def norm_of(dec_ref):
    lat, width = dec_ref.shape
    total = jnp.zeros((lat, LANES), F32)
    for c in range(0, width, LANES):
        part = dec_ref[:, c : c + LANES].astype(F32)
        total = total + part * part
    return jnp.sqrt(jnp.sum(total, axis=1, keepdims=True) + epsilon)


def norms_kernel(dec_ref, dec2_ref, codes_ref, codes2_ref, norm_ref, tail_ref):
    lat = dec_ref.shape[0]
    penalty = jnp.zeros((1, 1), F32)
    for k, (dec, codes) in enumerate(((dec_ref, codes_ref), (dec2_ref, codes2_ref))):
        norm = norm_of(dec)
        if k == 0:
            norm_ref[...] = norm
        by_lat = jnp.transpose(jnp.broadcast_to(norm, (lat, LANES)))[:1]
        each = jnp.sum(codes[...].astype(F32), axis=0, keepdims=True) * by_lat
        penalty = penalty + jnp.sum(each, axis=1, keepdims=True)
    tail_ref[...] = jnp.broadcast_to(penalty, tail_ref.shape)


def share_kernel(*refs):
    terms, (tail_ref, out_ref) = refs[:-2], refs[-2:]
    width = terms[0].shape[1]
    total = terms[0][...]
    for term in terms[1:]:
        total = total + term[...]
    out_ref[:, :width] = total
    out_ref[:, width:] = tail_ref[...]


def ready_kernel(codes_ref, others_ref, dec_ref, norm_ref, by_lat_ref, scale_ref, turned_ref, row_ref):
    lat, width = dec_ref.shape
    codes = jnp.transpose(jnp.concatenate([r[...].astype(F32) for r in (codes_ref, others_ref)]))
    by_lat_ref[...] = codes.astype(BF16)
    norm = norm_ref[...]
    scale_ref[...] = jnp.sum(codes, axis=1, keepdims=True) / norm
    row_ref[...] = jnp.transpose(jnp.broadcast_to(norm, (lat, LANES)))[:1]
    chunk = chunk_of(width)
    for c in range(0, width, chunk):
        turned_ref[c : c + chunk, :] = jnp.transpose(dec_ref[:, c : c + chunk])


def recon_of(terms, bias_ref):
    total = tree_sum([t[...] for t in terms])
    width = bias_ref.shape[1]
    return total[:, :width] + bias_ref[...], total[:1, width:]


def recon_kernel(n_terms, *refs):
    terms, (bias_ref, recon_ref) = refs[:n_terms], refs[n_terms:]
    recon_ref[...] = recon_of(terms, bias_ref)[0]


def error_kernel(n_terms, *refs):
    terms, (bias_ref, resid_ref, out_ref, pack) = refs[:n_terms], refs[n_terms:]
    rows, width = resid_ref.shape
    cut, piece = width // 2, width // rows
    recon, penalty = recon_of(terms, bias_ref)
    errors = recon - resid_ref[...].astype(F32)
    column = jnp.sum(errors, axis=0, keepdims=True)
    squares = jnp.zeros((rows, LANES), F32)
    for c in range(0, width, LANES):
        squares = squares + errors[:, c : c + LANES] * errors[:, c : c + LANES]
    value = 0.5 * jnp.sum(squares, axis=0, keepdims=True) + penalty * (1.0 / LANES)
    pack[:rows, :cut] = errors[:, :cut]
    pack[rows:, :cut] = errors[:, cut:]
    high = column.astype(BF16).astype(F32)
    low = column - high
    for r in range(rows):
        pack[r : r + 1, cut : cut + piece] = high[:, r * piece : (r + 1) * piece]
        pack[rows + r : rows + r + 1, cut : cut + piece] = low[:, r * piece : (r + 1) * piece]
    pack[:, cut + piece :] = jnp.zeros((2 * rows, LANES), F32)
    for r in range(3):
        high = value.astype(BF16).astype(F32)
        pack[r : r + 1, cut + piece :] = high
        value = value - high
    out_ref[...] = pack[...].astype(BF16)


def backward_kernel(
    order, near_ref, other_ref, codes_ref, scale_ref, dec_ref, turned_ref, norm_ref,
    grad_ref, code_grad_ref, column_ref, loss_ref,
    errors_ref, staged, by_row_ref, column_buf, loss_buf, sems, small_sems,
):
    half, rows2, _ = near_ref.shape
    rows = rows2 // 2
    lat, width = dec_ref.shape
    cut, piece = width // 2, width // rows
    blocks = [near_ref.at[p] if p < half else other_ref.at[p - half] for p in range(2 * half)]
    codes, scale = codes_ref[...], scale_ref[...]
    n_chunks, _, chunk = staged.shape
    copies = []

    def write(source, target, sem):
        copies.append(pltpu.make_async_copy(source, target, sem))
        copies[-1].start()

    def write_grad(i):
        cols = slice(i * chunk, (i + 1) * chunk)
        grad = contract(codes, errors_ref[:, cols], ((1,), (0,)))
        staged[i] = (grad + scale * dec_ref[:, cols].astype(F32)).astype(BF16)
        write(staged.at[i], grad_ref.at[:, cols], sems.at[i])

    for i in range(n_chunks):
        low = i * chunk % cut
        first = rows * (i * chunk // cut)
        part = [b[:, low : low + chunk].astype(F32)[first : first + rows] for b in blocks]
        errors_ref[:, i * chunk : (i + 1) * chunk] = jnp.concatenate(part).astype(BF16)
    for i in range(n_chunks // 2):
        write_grad(i)

    by_row = jnp.broadcast_to(norm_ref[...], (2 * half * rows, lat))
    step = chunk_of(width)
    for c in range(0, width, step):
        by_row = by_row + contract(errors_ref[:, c : c + step], turned_ref[c : c + step], ((1,), (0,)))
    me = lax.axis_index("tensor")
    for p, mask in enumerate(order[:half]):
        block = lax.bitwise_xor(me, mask)
        one = by_row[p * rows : (p + 1) * rows]
        two = by_row[(half + p) * rows : (half + p + 1) * rows]
        if len(by_row_ref.shape) == 3:
            by_row_ref[block] = one
            by_row_ref[lax.bitwise_xor(block, 1)] = two
        else:
            odd = lax.rem(block, 2) == 1
            both = jnp.concatenate([jnp.where(odd, two, one), jnp.where(odd, one, two)])
            start = pl.multiple_of(lax.div(block, 2) * 2 * rows, 2 * rows)
            by_row_ref[pl.ds(start, 2 * rows), :] = both
    write(by_row_ref, code_grad_ref, small_sems.at[0])
    for i in range(n_chunks // 2, n_chunks):
        write_grad(i)

    columns, losses = {}, {}
    for p, mask in enumerate(order):
        ends = blocks[p][:, cut:].astype(F32)
        columns[mask] = ends[:rows, :piece] + ends[rows:, :piece]
        losses[mask] = (ends[0:1, piece:] + ends[1:2, piece:]) + ends[2:3, piece:]
    column = tree_sum([columns[m] for m in range(len(order))])
    for r in range(rows):
        column_buf[r * piece : (r + 1) * piece] = column[r]
    write(column_buf, column_ref, small_sems.at[1])
    loss = tree_sum([losses[m] for m in range(len(order))])
    loss_buf[...] = jnp.sum(loss, axis=1, keepdims=True) / (len(order) * rows * width)
    write(loss_buf, loss_ref, small_sems.at[2])
    for copy in copies:
        copy.wait()


def per_device(n_section, n_tensor, resid, w_enc, b_enc, w_dec, b_dec):
    rows, width = resid.shape
    lat = w_enc.shape[0]
    masks = far_masks(n_tensor)
    order = masks + [m ^ 1 for m in masks]
    half = len(masks)
    total_rows = n_tensor * rows
    wide = width + LANES
    shape = jax.ShapeDtypeStruct

    anywhere = pl.BlockSpec(memory_space=pl.ANY)
    anywhere = pl.BlockSpec(memory_space=pl.ANY)
    bias = b_enc.reshape(1, lat)
    stored = [pltpu.with_memory_space_constraint(x, pltpu.HBM) for x in (w_dec, w_enc, bias, resid)]

    def mate(x):
        return swaps([x], "tensor", n_tensor, [1])[0]

    def call(kernel, outs, *args, **kwargs):
        return pl.pallas_call(
            kernel,
            out_shape=tuple(outs),
            in_specs=[VMEM] * len(args),
            out_specs=(VMEM,) * len(outs),
            compiler_params=PARAMS,
            **kwargs,
        )(*args)

    enc2, dec2, bias2 = mate(w_enc), mate(w_dec), mate(bias)
    w_dec, w_enc, bias, own = pl.pallas_call(
        fetch_kernel,
        out_shape=tuple(shape(x.shape, x.dtype) for x in (w_dec, w_enc, bias, resid)),
        in_specs=[anywhere] * 4,
        out_specs=(VMEM,) * 4,
        compiler_params=PARAMS,
        scratch_shapes=[pltpu.SemaphoreType.DMA((4,))],
    )(*stored)
    blocks = [own] + swaps([resid] * half, "tensor", n_tensor, masks[1:])
    part, codes, codes2 = call(
        functools.partial(forward_kernel, half),
        [shape((half * rows, width), F32)] + [shape((half * rows, lat), BF16)] * 2,
        *blocks, w_enc, enc2, bias, bias2, w_dec,
    )
    shares = call(mate_kernel, [shape((rows, width), F32)] * half, part, codes2, dec2)
    received = swaps(shares[1:], "tensor", n_tensor, masks[1:])
    norm, tail = call(
        norms_kernel,
        [shape((lat, 1), F32), shape((rows, LANES), F32)],
        w_dec, dec2, codes, codes2,
    )
    (share,) = call(share_kernel, [shape((rows, wide), F32)], shares[0], *received, tail)
    across = range(1, n_section)
    terms = [share] + swaps([share] * n_section, "section", n_section, across)
    by_lat, scale, turned, norm = call(
        ready_kernel,
        [
            shape((lat, total_rows), BF16),
            shape((lat, 1), F32),
            shape((width, lat), BF16),
            shape((1, lat), F32),
        ],
        codes, mate(codes2), w_dec, norm,
    )
    packed = width // 2 + width // rows + LANES
    bias = b_dec.reshape(1, width)
    payload = pl.pallas_call(
        functools.partial(error_kernel, len(terms)),
        out_shape=shape((2 * rows, packed), BF16),
        in_specs=[VMEM] * (len(terms) + 2),
        out_specs=VMEM,
        compiler_params=PARAMS,
        scratch_shapes=[pltpu.VMEM((2 * rows, packed), F32)],
    )(*terms, bias, own)
    near = jnp.stack([payload] + swaps([payload] * half, "tensor", n_tensor, masks[1:]))
    recon = pl.pallas_call(
        functools.partial(recon_kernel, len(terms)),
        out_shape=shape((rows, width), F32),
        in_specs=[VMEM] * (len(terms) + 1),
        out_specs=VMEM,
        compiler_params=PARAMS,
    )(*terms, bias)
    other = swap(near, "tensor", n_tensor, 1)
    chunk = width // 4
    n_chunks = width // chunk
    by_row = (total_rows, lat) if rows % 4 == 0 else (n_tensor, rows, lat)
    grad_w_dec, code_grad, column, loss = pl.pallas_call(
        functools.partial(backward_kernel, order),
        out_shape=(
            shape((lat, width), BF16),
            shape(by_row, F32),
            shape((width,), F32),
            shape((1, 1), F32),
        ),
        in_specs=[VMEM] * 7,
        out_specs=(anywhere,) * 4,
        compiler_params=PARAMS,
        scratch_shapes=[
            pltpu.VMEM((total_rows, width), BF16),
            pltpu.VMEM((n_chunks, lat, chunk), BF16),
            pltpu.VMEM(by_row, F32),
            pltpu.VMEM((width,), F32),
            pltpu.VMEM((1, 1), F32),
            pltpu.SemaphoreType.DMA((n_chunks,)),
            pltpu.SemaphoreType.DMA((3,)),
        ],
    )(near, other, by_lat, scale, w_dec, turned, norm)
    return recon, grad_w_dec, code_grad.reshape(total_rows, lat), column, loss.reshape(())


def solution(mesh):
    n_section, n_tensor = mesh.shape["section"], mesh.shape["tensor"]
    in_specs = (
        P("tensor", None),
        P(("section", "tensor"), None),
        P(("section", "tensor")),
        P(("section", "tensor"), None),
        P(),
    )
    out_specs = (
        P("tensor", None),
        P(("section", "tensor"), None),
        P(None, ("section", "tensor")),
        P(),
        P(),
    )

    def body(*args):
        return per_device(n_section, n_tensor, *args)

    return jax.shard_map(body, mesh=mesh, in_specs=in_specs, out_specs=out_specs, check_vma=False)
```

time: 39.2 us -> 42.6 us (1.087)
  starting transfers between devices: 14.5 us -> 18.4 us
  waiting for transfers between devices: 17.3 us -> 15.6 us
  Pallas kernels: 6.18 us -> 7.6 us
    ppermute x15 -> x17, starting transfers between devices: 14.5 us -> 18.4 us  [swap(): return lax.ppermute(x, axis, [(i, i ^ mask) for i in range(size)])]
    ppermute x15 -> x17, waiting for transfers between devices: 17.3 us -> 15.6 us  [swap(): return lax.ppermute(x, axis, [(i, i ^ mask) for i in range(size)])]
    pallas_call x4 -> x7, Pallas kernels: 3.71 us -> 5.32 us  [the longest x5 3.27 us: call(): pl.pallas_call(kernel, out_shape=tuple(outs), in_specs=[VMEM] * len(args)...]
  transfers between devices with their start and end apart: 15 -> 17, of which waited for: 12 -> 8; matrix products, arithmetic and copies ran while one was open for 0% -> 0% of each run, Pallas kernels for 8% -> 13%
where the time goes in v2:
time: 42.6 us; the launch traced here: 42.4 us
  starting transfers between devices  18.4 us (43%)
  waiting for transfers between devices  15.6 us (37%)
  Pallas kernels  7.6 us (18%)
  between operations  0.72 us (2%)
    ppermute x17, starting transfers between devices, swap(): return lax.ppermute(x, axis, [(i, i ^ mask) for i in range(size)])  18.4 us
    ppermute x17, waiting for transfers between devices, swap(): return lax.ppermute(x, axis, [(i, i ^ mask) for i in range(size)])  15.6 us
    pallas_call x5, Pallas kernels, call(): pl.pallas_call(kernel, out_shape=tuple(outs), in_specs=[VMEM] * len(args)...  3.27 us
    pallas_call x1, Pallas kernels, per_device(): pl.pallas_call(fetch_kernel, out_shape=tuple((shape(x.shape, x.dtype) for...  1.94 us
    pallas_call x1, Pallas kernels, per_device(): pl.pallas_call(functools.partial(backward_kernel, order), out_shape=(shap...  1.64 us
  transfers between devices with their start and end apart: 17, of which 8 were waited for; matrix products, arithmetic and copies ran while one was open for 0% of the time, Pallas kernels for 13%

profile of v2, /device:TPU:0, one launch (start us, length us, event | category | flops | bytes accessed | tf_op | source)
XLA Modules:
  0.0 42.4 jit_solution(298147261414153672)
XLA Ops:
  0.6 0.6 %collective-permute-start.3 = (bf16[224,3584]{1,0:T(8,128)(2,1)}, bf16[224,3584]{1,0:T(8,128)(2,1)S(1)}, u32[]{:S(2)}, u32[]{:S(2)}) collective-permute-start(bf16[224,3584]{1,0:T(8,128)(2,1)} %enc_hbm.1), channel_id=1, source_target_pairs={{0,1},{1,0},{2,3},{3,2},{4,5},{5,4},{6,7},{7,6},{8,9},{9,8},{10,11... | collective-permute-start | bytes 4816904 | tf_op jit(solution)/shard_map/ppermute | solution.py:21
  1.2 0.1 collective-permute-start.5
  1.3 0.4 %collective-permute-start.4 = (f32[1,224]{1,0:T(1,128)}, f32[1,224]{1,0:T(1,128)S(1)}, u32[]{:S(2)}, u32[]{:S(2)}) collective-permute-start(f32[1,224]{1,0:T(1,128)} %bitcast.10), channel_id=1, source_target_pairs={{0,1},{1,0},{2,3},{3,2},{4,5},{5,4},{6,7},{7,6},{8,9},{9,8},{10,11... | collective-permute-start | bytes 2696 | tf_op jit(solution)/shard_map/ppermute | solution.py:21
  1.7 2.6 %collective-permute-start = (bf16[4,3584]{1,0:T(4,128)(2,1)}, bf16[4,3584]{1,0:T(4,128)(2,1)S(1)}, u32[]{:S(2)}, u32[]{:S(2)}) collective-permute-start(bf16[4,3584]{1,0:T(4,128)(2,1)} %resid_hbm.1), channel_id=1, source_target_pairs={{0,3},{1,2},{2,1},{3,0},{4,7},{5,6},{6,5},{7,4},{8,11},{9,10},{10,... | collective-permute-start | bytes 86024 | tf_op jit(solution)/shard_map/ppermute | solution.py:21
  4.3 1.2 %collective-permute-start.1 = (bf16[4,3584]{1,0:T(4,128)(2,1)}, bf16[4,3584]{1,0:T(4,128)(2,1)S(1)}, u32[]{:S(2)}, u32[]{:S(2)}) collective-permute-start(bf16[4,3584]{1,0:T(4,128)(2,1)} %resid_hbm.1), channel_id=1, source_target_pairs={{0,5},{1,4},{2,7},{3,6},{4,1},{5,0},{6,3},{7,2},{8,13},{9,12},{10,... | collective-permute-start | bytes 86024 | tf_op jit(solution)/shard_map/ppermute | solution.py:21
  5.5 1.3 %collective-permute-done.4.refs_7_ = f32[1,224]{1,0:T(1,128)S(1)} collective-permute-done((f32[1,224]{1,0:T(1,128)}, f32[1,224]{1,0:T(1,128)S(1)}, u32[]{:S(2)}, u32[]{:S(2)}) %collective-permute-start.4) | collective-permute-done | bytes 928 | tf_op jit(solution)/shard_map/ppermute | solution.py:21
  6.8 3.5 %collective-permute-start.2 = (bf16[4,3584]{1,0:T(4,128)(2,1)}, bf16[4,3584]{1,0:T(4,128)(2,1)S(1)}, u32[]{:S(2)}, u32[]{:S(2)}) collective-permute-start(bf16[4,3584]{1,0:T(4,128)(2,1)} %resid_hbm.1), channel_id=1, source_target_pairs={{0,7},{1,6},{2,5},{3,4},{4,3},{5,2},{6,1},{7,0},{8,15},{9,14},{10,... | collective-permute-start | bytes 86024 | tf_op jit(solution)/shard_map/ppermute | solution.py:21
  10.3 1.9 %shard_map.92 = (bf16[224,3584]{1,0:T(8,128)(2,1)S(1)}, bf16[224,3584]{1,0:T(8,128)(2,1)S(1)}, f32[1,224]{1,0:T(1,128)S(1)}, bf16[4,3584]{1,0:T(4,128)(2,1)S(1)}) custom-call(bf16[224,3584]{1,0:T(8,128)(2,1)} %dec_hbm.1, bf16[224,3584]{1,0:T(8,128)(2,1)} %enc_hbm.1, f32[1,224]{1,0:T(1,128)} %bitcast.11, bf16[4,3584]{1,0:T(4,128)(2,1)} %resid_hbm.1), custom_call_target="tpu_custom_call" | custom-call | tf_op jit(solution)/shard_map/pallas_call | solution.py:267
  12.3 0.0 collective-permute-done.refs_1_
  12.3 0.0 collective-permute-done.1.refs_2_
  12.3 0.0 collective-permute-done.2.refs_3_
  12.3 0.0 collective-permute-done.3.refs_5_
  12.3 1.3 %shard_map.93 = (f32[16,3584]{1,0:T(8,128)S(1)}, bf16[16,224]{1,0:T(8,128)(2,1)S(1)}, bf16[16,224]{1,0:T(8,128)(2,1)S(1)}) custom-call(bf16[4,3584]{1,0:T(4,128)(2,1)S(1)} %get-tuple-element.26.refs_0_.refs_5_, bf16[4,3584]{1,0:T(4,128)(2,1)S(1)} %collective-permute-done.refs_1_, bf16[4,3584]{1,0:T(4,128)(2,1)S(1)} %collective-permute-done.1.refs_2_, ...), custom_call_target="tpu_custom_call" | custom-call | tf_op jit(solution)/shard_map/pallas_call | solution.py:257
  13.6 0.0 collective-permute-done.5.dec_ref.dec2_ref
  13.6 0.3 shard_map.94
  14.0 1.5 %collective-permute-start.6 = (f32[4,3584]{1,0:T(4,128)S(1)}, f32[4,3584]{1,0:T(4,128)S(1)}, u32[]{:S(2)}, u32[]{:S(2)}) collective-permute-start(f32[4,3584]{1,0:T(4,128)S(1)} %get-tuple-element.33), channel_id=1, source_target_pairs={{0,3},{1,2},{2,1},{3,0},{4,7},{5,6},{6,5},{7,4},{8,11},{9,10},{10,... | collective-permute-start | bytes 172040 | tf_op jit(solution)/shard_map/ppermute | solution.py:21
  15.5 1.5 %collective-permute-start.7 = (f32[4,3584]{1,0:T(4,128)S(1)}, f32[4,3584]{1,0:T(4,128)S(1)}, u32[]{:S(2)}, u32[]{:S(2)}) collective-permute-start(f32[4,3584]{1,0:T(4,128)S(1)} %get-tuple-element.34), channel_id=1, source_target_pairs={{0,5},{1,4},{2,7},{3,6},{4,1},{5,0},{6,3},{7,2},{8,13},{9,12},{10,... | collective-permute-start | bytes 172040 | tf_op jit(solution)/shard_map/ppermute | solution.py:21
  17.0 0.2 collective-permute-start.8
  17.2 0.0 copy-start
  17.2 0.8 %shard_map.95 = (f32[224,1]{1,0:T(8,128)S(1)}, f32[4,128]{1,0:T(4,128)S(1)}) custom-call(bf16[224,3584]{1,0:T(8,128)(2,1)S(1)} %get-tuple-element.29.refs_8_.dec_ref, bf16[224,3584]{1,0:T(8,128)(2,1)S(1)} %collective-permute-done.5.dec_ref.dec2_ref, bf16[16,224]{1,0:T(8,128)(2,1)S(1)} %get-tuple-element.36.codes_ref, ...), custom_call_target="tpu_custom_call" | custom-call | tf_op jit(solution)/shard_map/pallas_call | solution.py:257
  18.0 0.0 collective-permute-done.6.refs_1_
  18.0 1.1 %collective-permute-done.7.refs_2_ = f32[4,3584]{1,0:T(4,128)S(1)} collective-permute-done((f32[4,3584]{1,0:T(4,128)S(1)}, f32[4,3584]{1,0:T(4,128)S(1)}, u32[]{:S(2)}, u32[]{:S(2)}) %collective-permute-start.7) | collective-permute-done | bytes 57376 | tf_op jit(solution)/shard_map/ppermute | solution.py:21
  19.1 2.6 %collective-permute-done.8.refs_3_ = f32[4,3584]{1,0:T(4,128)S(1)} collective-permute-done((f32[4,3584]{1,0:T(4,128)S(1)}, f32[4,3584]{1,0:T(4,128)S(1)}, u32[]{:S(2)}, u32[]{:S(2)}) %collective-permute-start.8) | collective-permute-done | bytes 57376 | tf_op jit(solution)/shard_map/ppermute | solution.py:21
  21.8 1.6 %collective-permute-start.9 = (f32[4,3712]{1,0:T(4,128)S(1)}, f32[4,3712]{1,0:T(4,128)S(1)}, u32[]{:S(2)}, u32[]{:S(2)}) collective-permute-start(f32[4,3712]{1,0:T(4,128)S(1)} %shard_map.96.refs_0_), channel_id=1, source_target_pairs={{0,8},{8,0},{16,24},{24,16},{1,9},{9,1},{17,25},{25,17},{2,10},{10... | collective-permute-start | bytes 178184 | tf_op jit(solution)/shard_map/ppermute | solution.py:21
  23.4 2.6 %collective-permute-start.10 = (f32[4,3712]{1,0:T(4,128)S(1)}, f32[4,3712]{1,0:T(4,128)S(1)}, u32[]{:S(2)}, u32[]{:S(2)}) collective-permute-start(f32[4,3712]{1,0:T(4,128)S(1)} %shard_map.96.refs_0_), channel_id=1, source_target_pairs={{0,16},{8,24},{16,0},{24,8},{1,17},{9,25},{17,1},{25,9},{2,18},{10... | collective-permute-start | bytes 178184 | tf_op jit(solution)/shard_map/ppermute | solution.py:21
  26.0 0.2 collective-permute-start.11
  26.2 0.0 copy-done
  26.3 0.0 collective-permute-done.9.refs_1_
  26.3 3.7 %collective-permute-done.10.refs_2_ = f32[4,3712]{1,0:T(4,128)S(1)} collective-permute-done((f32[4,3712]{1,0:T(4,128)S(1)}, f32[4,3712]{1,0:T(4,128)S(1)}, u32[]{:S(2)}, u32[]{:S(2)}) %collective-permute-start.10) | collective-permute-done | bytes 59424 | tf_op jit(solution)/shard_map/ppermute | solution.py:21
  29.9 2.1 %collective-permute-done.11.refs_3_ = f32[4,3712]{1,0:T(4,128)S(1)} collective-permute-done((f32[4,3712]{1,0:T(4,128)S(1)}, f32[4,3712]{1,0:T(4,128)S(1)}, u32[]{:S(2)}, u32[]{:S(2)}) %collective-permute-start.11) | collective-permute-done | bytes 59424 | tf_op jit(solution)/shard_map/ppermute | solution.py:21
  32.0 0.1 shard_map.98
  32.1 0.1 collective-permute-start.14
  32.2 1.7 %collective-permute-start.13 = (bf16[8,2816]{1,0:T(8,128)(2,1)S(1)}, bf16[8,2816]{1,0:T(8,128)(2,1)S(1)}, u32[]{:S(2)}, u32[]{:S(2)}) collective-permute-start(bf16[8,2816]{1,0:T(8,128)(2,1)S(1)} %shard_map.98), channel_id=1, source_target_pairs={{0,5},{1,4},{2,7},{3,6},{4,1},{5,0},{6,3},{7,2},{8,13},{9,12},{10,... | collective-permute-start | bytes 135176 | tf_op jit(solution)/shard_map/ppermute | solution.py:21
  33.9 0.0 collective-permute-start.12
  33.9 2.8 %collective-permute-done.14 = bf16[8,2816]{1,0:T(8,128)(2,1)S(1)} collective-permute-done((bf16[8,2816]{1,0:T(8,128)(2,1)S(1)}, bf16[8,2816]{1,0:T(8,128)(2,1)S(1)}, u32[]{:S(2)}, u32[]{:S(2)}) %collective-permute-start.14) | collective-permute-done | bytes 45088 | tf_op jit(solution)/shard_map/ppermute | solution.py:21
  36.7 0.0 collective-permute-done.13
  36.7 1.1 %collective-permute-done.12 = bf16[8,2816]{1,0:T(8,128)(2,1)S(1)} collective-permute-done((bf16[8,2816]{1,0:T(8,128)(2,1)S(1)}, bf16[8,2816]{1,0:T(8,128)(2,1)S(1)}, u32[]{:S(2)}, u32[]{:S(2)}) %collective-permute-start.12) | collective-permute-done | bytes 45088 | tf_op jit(solution)/shard_map/ppermute | solution.py:21
  37.8 0.2 collective-permute-start.15
  38.0 0.4 collective-permute-start.16
  38.4 0.9 %collective-permute-done.16.others_ref = bf16[16,224]{1,0:T(8,128)(2,1)S(1)} collective-permute-done((bf16[16,224]{1,0:T(8,128)(2,1)S(1)}, bf16[16,224]{1,0:T(8,128)(2,1)S(1)}, u32[]{:S(2)}, u32[]{:S(2)}) %collective-permute-start.16) | collective-permute-done | bytes 7200 | tf_op jit(solution)/shard_map/ppermute | solution.py:21
  39.3 0.8 %shard_map.99 = (bf16[224,32]{1,0:T(8,128)(2,1)S(1)}, f32[224,1]{1,0:T(8,128)S(1)}, bf16[3584,224]{1,0:T(8,128)(2,1)S(1)}, f32[1,224]{1,0:T(1,128)S(1)}) custom-call(bf16[16,224]{1,0:T(8,128)(2,1)S(1)} %get-tuple-element.36.codes_ref, bf16[16,224]{1,0:T(8,128)(2,1)S(1)} %collective-permute-done.16.others_ref, ...), custom_call_target="tpu_custom_call" | custom-call | tf_op jit(solution)/shard_map/pallas_call | solution.py:257
  40.1 0.6 %shard_map.97 = f32[4,3584]{1,0:T(4,128)} custom-call(f32[4,3712]{1,0:T(4,128)S(1)} %shard_map.96.refs_0_, f32[4,3712]{1,0:T(4,128)S(1)} %collective-permute-done.9.refs_1_, f32[4,3712]{1,0:T(4,128)S(1)} %collective-permute-done.10.refs_2_, f32[4,3712]{1,0:T(4,128)S(1)} %collective-permute-done.11.refs_3_, f32[1,3584]{1,0:T(1,128)S(1)} %reshape.20.refs_4_), custom_call_target="tpu_custom_call" | custom-call | tf_op jit(solution)/shard_map/pallas_call | solution.py:312
  40.8 0.0 collective-permute-done.15.other_ref
  40.8 1.6 %shard_map.100 = (bf16[224,3584]{1,0:T(8,128)(2,1)}, f32[32,224]{1,0:T(8,128)}, f32[3584]{0:T(1024)}, f32[1,1]{1,0:T(1,128)}) custom-call(bf16[4,8,2816]{2,1,0:T(8,128)(2,1)S(1)} %pad_maximum_fusion.near_ref, bf16[4,8,2816]{2,1,0:T(8,128)(2,1)S(1)} %collective-permute-done.15.other_ref, bf16[224,32]{1,0:T(8,128)(2,1)S(1)} %get-tuple-element.39.codes_ref, ...), custom_call_target="tpu_custom_call" | custom-call | tf_op jit(solution)/shard_map/pallas_call | solution.py:323
  (3 shorter events, 0.1 us)
Async XLA Ops:
  0.6 11.7 %collective-permute-start.3 = (bf16[224,3584]{1,0:T(8,128)(2,1)}, bf16[224,3584]{1,0:T(8,128)(2,1)S(1)}, u32[]{:S(2)}, u32[]{:S(2)}) collective-permute-start(bf16[224,3584]{1,0:T(8,128)(2,1)} %enc_hbm.1), channel_id=1, source_target_pairs={{0,1},{1,0},{2,3},{3,2},{4,5},{5,4},{6,7},{7,6},{8,9},{9,8},{10,11... | collective-permute-start | bytes 4816904 | tf_op jit(solution)/shard_map/ppermute | solution.py:21
  1.2 12.4 %collective-permute-start.5 = (bf16[224,3584]{1,0:T(8,128)(2,1)}, bf16[224,3584]{1,0:T(8,128)(2,1)S(1)}, u32[]{:S(2)}, u32[]{:S(2)}) collective-permute-start(bf16[224,3584]{1,0:T(8,128)(2,1)} %dec_hbm.1), channel_id=1, source_target_pairs={{0,1},{1,0},{2,3},{3,2},{4,5},{5,4},{6,7},{7,6},{8,9},{9,8},{10,11... | collective-permute-start | bytes 4816904 | tf_op jit(solution)/shard_map/ppermute | solution.py:21
  1.3 5.5 %collective-permute-start.4 = (f32[1,224]{1,0:T(1,128)}, f32[1,224]{1,0:T(1,128)S(1)}, u32[]{:S(2)}, u32[]{:S(2)}) collective-permute-start(f32[1,224]{1,0:T(1,128)} %bitcast.10), channel_id=1, source_target_pairs={{0,1},{1,0},{2,3},{3,2},{4,5},{5,4},{6,7},{7,6},{8,9},{9,8},{10,11... | collective-permute-start | bytes 2696 | tf_op jit(solution)/shard_map/ppermute | solution.py:21
  1.7 10.6 %collective-permute-start = (bf16[4,3584]{1,0:T(4,128)(2,1)}, bf16[4,3584]{1,0:T(4,128)(2,1)S(1)}, u32[]{:S(2)}, u32[]{:S(2)}) collective-permute-start(bf16[4,3584]{1,0:T(4,128)(2,1)} %resid_hbm.1), channel_id=1, source_target_pairs={{0,3},{1,2},{2,1},{3,0},{4,7},{5,6},{6,5},{7,4},{8,11},{9,10},{10,... | collective-permute-start | bytes 86024 | tf_op jit(solution)/shard_map/ppermute | solution.py:21
  4.3 8.0 %collective-permute-start.1 = (bf16[4,3584]{1,0:T(4,128)(2,1)}, bf16[4,3584]{1,0:T(4,128)(2,1)S(1)}, u32[]{:S(2)}, u32[]{:S(2)}) collective-permute-start(bf16[4,3584]{1,0:T(4,128)(2,1)} %resid_hbm.1), channel_id=1, source_target_pairs={{0,5},{1,4},{2,7},{3,6},{4,1},{5,0},{6,3},{7,2},{8,13},{9,12},{10,... | collective-permute-start | bytes 86024 | tf_op jit(solution)/shard_map/ppermute | solution.py:21
  6.8 5.5 %collective-permute-start.2 = (bf16[4,3584]{1,0:T(4,128)(2,1)}, bf16[4,3584]{1,0:T(4,128)(2,1)S(1)}, u32[]{:S(2)}, u32[]{:S(2)}) collective-permute-start(bf16[4,3584]{1,0:T(4,128)(2,1)} %resid_hbm.1), channel_id=1, source_target_pairs={{0,7},{1,6},{2,5},{3,4},{4,3},{5,2},{6,1},{7,0},{8,15},{9,14},{10,... | collective-permute-start | bytes 86024 | tf_op jit(solution)/shard_map/ppermute | solution.py:21
  14.0 4.0 %collective-permute-start.6 = (f32[4,3584]{1,0:T(4,128)S(1)}, f32[4,3584]{1,0:T(4,128)S(1)}, u32[]{:S(2)}, u32[]{:S(2)}) collective-permute-start(f32[4,3584]{1,0:T(4,128)S(1)} %get-tuple-element.33), channel_id=1, source_target_pairs={{0,3},{1,2},{2,1},{3,0},{4,7},{5,6},{6,5},{7,4},{8,11},{9,10},{10,... | collective-permute-start | bytes 172040 | tf_op jit(solution)/shard_map/ppermute | solution.py:21
  15.5 3.7 %collective-permute-start.7 = (f32[4,3584]{1,0:T(4,128)S(1)}, f32[4,3584]{1,0:T(4,128)S(1)}, u32[]{:S(2)}, u32[]{:S(2)}) collective-permute-start(f32[4,3584]{1,0:T(4,128)S(1)} %get-tuple-element.34), channel_id=1, source_target_pairs={{0,5},{1,4},{2,7},{3,6},{4,1},{5,0},{6,3},{7,2},{8,13},{9,12},{10,... | collective-permute-start | bytes 172040 | tf_op jit(solution)/shard_map/ppermute | solution.py:21
  17.0 4.8 %collective-permute-start.8 = (f32[4,3584]{1,0:T(4,128)S(1)}, f32[4,3584]{1,0:T(4,128)S(1)}, u32[]{:S(2)}, u32[]{:S(2)}) collective-permute-start(f32[4,3584]{1,0:T(4,128)S(1)} %get-tuple-element.35), channel_id=1, source_target_pairs={{0,7},{1,6},{2,5},{3,4},{4,3},{5,2},{6,1},{7,0},{8,15},{9,14},{10,... | collective-permute-start | bytes 172040 | tf_op jit(solution)/shard_map/ppermute | solution.py:21
  17.2 9.0 %copy-start = (f32[3584]{0:T(1024)S(1)}, f32[3584]{0:T(1024)}, u32[]{:S(2)}) copy-start(f32[3584]{0:T(1024)} %param.9) | copy-start | bytes 43012
  21.8 4.5 %collective-permute-start.9 = (f32[4,3712]{1,0:T(4,128)S(1)}, f32[4,3712]{1,0:T(4,128)S(1)}, u32[]{:S(2)}, u32[]{:S(2)}) collective-permute-start(f32[4,3712]{1,0:T(4,128)S(1)} %shard_map.96.refs_0_), channel_id=1, source_target_pairs={{0,8},{8,0},{16,24},{24,16},{1,9},{9,1},{17,25},{25,17},{2,10},{10... | collective-permute-start | bytes 178184 | tf_op jit(solution)/shard_map/ppermute | solution.py:21
  23.4 6.5 %collective-permute-start.10 = (f32[4,3712]{1,0:T(4,128)S(1)}, f32[4,3712]{1,0:T(4,128)S(1)}, u32[]{:S(2)}, u32[]{:S(2)}) collective-permute-start(f32[4,3712]{1,0:T(4,128)S(1)} %shard_map.96.refs_0_), channel_id=1, source_target_pairs={{0,16},{8,24},{16,0},{24,8},{1,17},{9,25},{17,1},{25,9},{2,18},{10... | collective-permute-start | bytes 178184 | tf_op jit(solution)/shard_map/ppermute | solution.py:21
  26.0 6.0 %collective-permute-start.11 = (f32[4,3712]{1,0:T(4,128)S(1)}, f32[4,3712]{1,0:T(4,128)S(1)}, u32[]{:S(2)}, u32[]{:S(2)}) collective-permute-start(f32[4,3712]{1,0:T(4,128)S(1)} %shard_map.96.refs_0_), channel_id=1, source_target_pairs={{0,24},{8,16},{16,8},{24,0},{1,25},{9,17},{17,9},{25,1},{2,26},{10... | collective-permute-start | bytes 178184 | tf_op jit(solution)/shard_map/ppermute | solution.py:21
  32.1 4.5 %collective-permute-start.14 = (bf16[8,2816]{1,0:T(8,128)(2,1)S(1)}, bf16[8,2816]{1,0:T(8,128)(2,1)S(1)}, u32[]{:S(2)}, u32[]{:S(2)}) collective-permute-start(bf16[8,2816]{1,0:T(8,128)(2,1)S(1)} %shard_map.98), channel_id=1, source_target_pairs={{0,7},{1,6},{2,5},{3,4},{4,3},{5,2},{6,1},{7,0},{8,15},{9,14},{10,... | collective-permute-start | bytes 135176 | tf_op jit(solution)/shard_map/ppermute | solution.py:21
  32.2 4.5 %collective-permute-start.13 = (bf16[8,2816]{1,0:T(8,128)(2,1)S(1)}, bf16[8,2816]{1,0:T(8,128)(2,1)S(1)}, u32[]{:S(2)}, u32[]{:S(2)}) collective-permute-start(bf16[8,2816]{1,0:T(8,128)(2,1)S(1)} %shard_map.98), channel_id=1, source_target_pairs={{0,5},{1,4},{2,7},{3,6},{4,1},{5,0},{6,3},{7,2},{8,13},{9,12},{10,... | collective-permute-start | bytes 135176 | tf_op jit(solution)/shard_map/ppermute | solution.py:21
  33.9 3.9 %collective-permute-start.12 = (bf16[8,2816]{1,0:T(8,128)(2,1)S(1)}, bf16[8,2816]{1,0:T(8,128)(2,1)S(1)}, u32[]{:S(2)}, u32[]{:S(2)}) collective-permute-start(bf16[8,2816]{1,0:T(8,128)(2,1)S(1)} %shard_map.98), channel_id=1, source_target_pairs={{0,3},{1,2},{2,1},{3,0},{4,7},{5,6},{6,5},{7,4},{8,11},{9,10},{10,... | collective-permute-start | bytes 135176 | tf_op jit(solution)/shard_map/ppermute | solution.py:21
  37.8 3.0 %collective-permute-start.15 = (bf16[4,8,2816]{2,1,0:T(8,128)(2,1)S(1)}, bf16[4,8,2816]{2,1,0:T(8,128)(2,1)S(1)}, u32[]{:S(2)}, u32[]{:S(2)}) collective-permute-start(bf16[4,8,2816]{2,1,0:T(8,128)(2,1)S(1)} %pad_maximum_fusion.near_ref), channel_id=1, source_target_pairs={{0,1},{1,0},{2,3},{3,2},{4,5},{5,4},{6,7},{7,6},{8,9},{9,8},{10,11... | collective-permute-start | bytes 540680 | tf_op jit(solution)/shard_map/ppermute | solution.py:21
  38.0 1.3 %collective-permute-start.16 = (bf16[16,224]{1,0:T(8,128)(2,1)S(1)}, bf16[16,224]{1,0:T(8,128)(2,1)S(1)}, u32[]{:S(2)}, u32[]{:S(2)}) collective-permute-start(bf16[16,224]{1,0:T(8,128)(2,1)S(1)} %get-tuple-element.31.codes_ref.codes2_ref), channel_id=1, source_target_pairs={{0,1},{1,0},{2,3},{3,2},{4,5},{5,4},{6,7},{7,6},{8,9},{9,8},{10,11... | collective-permute-start | bytes 21512 | tf_op jit(solution)/shard_map/ppermute | solution.py:21

commit v3 on v2

--- a/solution.py
+++ b/solution.py
@@ -57,8 +57,8 @@
 
 def forward_kernel(half, *refs):
     blocks, refs = refs[:half], refs[half:]
-    encs, biases, dec_ref = refs[0:2], refs[2:4], refs[4]
-    part_ref, codes_refs = refs[5], refs[6:]
+    encs, biases, decs = refs[0:2], refs[2:4], refs[4:6]
+    shares, codes_refs = refs[6 : 6 + half], refs[6 + half :]
     rows, width = blocks[0].shape
     lat = encs[0].shape[0]
     chunk = chunk_of(width)
@@ -72,17 +72,10 @@
         codes_ref[...] = jnp.maximum(preact, 0.0).astype(BF16)
     for c in range(0, width, chunk):
         cols = slice(c, c + chunk)
-        part_ref[:, cols] = contract(codes_refs[0][...], dec_ref[:, cols], ((1,), (0,)))
-
-
-def mate_kernel(part_ref, codes_ref, dec_ref, *shares):
-    rows, width = shares[0].shape
-    chunk = chunk_of(width)
-    for c in range(0, width, chunk):
-        cols = slice(c, c + chunk)
-        total = part_ref[:, cols] + contract(codes_ref[...], dec_ref[:, cols], ((1,), (0,)))
+        part = contract(codes_refs[0][...], decs[0][:, cols], ((1,), (0,)))
+        part = part + contract(codes_refs[1][...], decs[1][:, cols], ((1,), (0,)))
         for k, share in enumerate(shares):
-            share[:, cols] = total[k * rows : (k + 1) * rows]
+            share[:, cols] = part[k * rows : (k + 1) * rows]
 
 
 def norm_of(dec_ref):
@@ -273,12 +266,11 @@
         scratch_shapes=[pltpu.SemaphoreType.DMA((4,))],
     )(*stored)
     blocks = [own] + swaps([resid] * half, "tensor", n_tensor, masks[1:])
-    part, codes, codes2 = call(
+    *shares, codes, codes2 = call(
         functools.partial(forward_kernel, half),
-        [shape((half * rows, width), F32)] + [shape((half * rows, lat), BF16)] * 2,
-        *blocks, w_enc, enc2, bias, bias2, w_dec,
-    )
-    shares = call(mate_kernel, [shape((rows, width), F32)] * half, part, codes2, dec2)
+        [shape((rows, width), F32)] * half + [shape((half * rows, lat), BF16)] * 2,
+        *blocks, w_enc, enc2, bias, bias2, w_dec, dec2,
+    )
     received = swaps(shares[1:], "tensor", n_tensor, masks[1:])
     norm, tail = call(
         norms_kernel,

time: 42.6 us -> 40.8 us (0.958)
  waiting for transfers between devices: 15.6 us -> 14.1 us
    ppermute x17, waiting for transfers between devices: 15.6 us -> 14.1 us  [swap(): return lax.ppermute(x, axis, [(i, i ^ mask) for i in range(size)])]
    pallas_call x5 -> x4, Pallas kernels: 3.27 us -> 3.15 us  [call(): pl.pallas_call(kernel, out_shape=tuple(outs), in_specs=[VMEM] * len(args)...]
  transfers between devices with their start and end apart: 17 -> 17, of which waited for: 8 -> 10; matrix products, arithmetic and copies ran while one was open for 0% -> 0% of each run, Pallas kernels for 13% -> 10%
where the time goes in v3:
time: 40.8 us; the launch traced here: 40.6 us
  starting transfers between devices  18.2 us (45%)
  waiting for transfers between devices  14.1 us (35%)
  Pallas kernels  7.51 us (18%)
  between operations  0.72 us (2%)
    ppermute x17, starting transfers between devices, swap(): return lax.ppermute(x, axis, [(i, i ^ mask) for i in range(size)])  18.2 us
    ppermute x17, waiting for transfers between devices, swap(): return lax.ppermute(x, axis, [(i, i ^ mask) for i in range(size)])  14.1 us
    pallas_call x4, Pallas kernels, call(): pl.pallas_call(kernel, out_shape=tuple(outs), in_specs=[VMEM] * len(args)...  3.15 us
    pallas_call x1, Pallas kernels, per_device(): pl.pallas_call(fetch_kernel, out_shape=tuple((shape(x.shape, x.dtype) for...  1.94 us
    pallas_call x1, Pallas kernels, per_device(): pl.pallas_call(functools.partial(backward_kernel, order), out_shape=(shap...  1.65 us
  transfers between devices with their start and end apart: 17, of which 10 were waited for; matrix products, arithmetic and copies ran while one was open for 0% of the time, Pallas kernels for 10%

profile of v3, /device:TPU:0, one launch (start us, length us, event | category | flops | bytes accessed | tf_op | source)
XLA Modules:
  0.0 40.6 jit_solution(10999590608590917805)
XLA Ops:
  0.6 0.6 %collective-permute-start.5 = (bf16[224,3584]{1,0:T(8,128)(2,1)}, bf16[224,3584]{1,0:T(8,128)(2,1)S(1)}, u32[]{:S(2)}, u32[]{:S(2)}) collective-permute-start(bf16[224,3584]{1,0:T(8,128)(2,1)} %dec_hbm.1), channel_id=1, source_target_pairs={{0,1},{1,0},{2,3},{3,2},{4,5},{5,4},{6,7},{7,6},{8,9},{9,8},{10,11... | collective-permute-start | bytes 4816904 | tf_op jit(solution)/shard_map/ppermute | solution.py:21
  1.2 0.1 collective-permute-start.3
  1.3 0.4 %collective-permute-start.4 = (f32[1,224]{1,0:T(1,128)}, f32[1,224]{1,0:T(1,128)S(1)}, u32[]{:S(2)}, u32[]{:S(2)}) collective-permute-start(f32[1,224]{1,0:T(1,128)} %bitcast.10), channel_id=1, source_target_pairs={{0,1},{1,0},{2,3},{3,2},{4,5},{5,4},{6,7},{7,6},{8,9},{9,8},{10,11... | collective-permute-start | bytes 2696 | tf_op jit(solution)/shard_map/ppermute | solution.py:21
  1.7 2.6 %collective-permute-start = (bf16[4,3584]{1,0:T(4,128)(2,1)}, bf16[4,3584]{1,0:T(4,128)(2,1)S(1)}, u32[]{:S(2)}, u32[]{:S(2)}) collective-permute-start(bf16[4,3584]{1,0:T(4,128)(2,1)} %resid_hbm.1), channel_id=1, source_target_pairs={{0,3},{1,2},{2,1},{3,0},{4,7},{5,6},{6,5},{7,4},{8,11},{9,10},{10,... | collective-permute-start | bytes 86024 | tf_op jit(solution)/shard_map/ppermute | solution.py:21
  4.3 1.2 %collective-permute-start.1 = (bf16[4,3584]{1,0:T(4,128)(2,1)}, bf16[4,3584]{1,0:T(4,128)(2,1)S(1)}, u32[]{:S(2)}, u32[]{:S(2)}) collective-permute-start(bf16[4,3584]{1,0:T(4,128)(2,1)} %resid_hbm.1), channel_id=1, source_target_pairs={{0,5},{1,4},{2,7},{3,6},{4,1},{5,0},{6,3},{7,2},{8,13},{9,12},{10,... | collective-permute-start | bytes 86024 | tf_op jit(solution)/shard_map/ppermute | solution.py:21
  5.5 1.3 %collective-permute-done.4.refs_7_ = f32[1,224]{1,0:T(1,128)S(1)} collective-permute-done((f32[1,224]{1,0:T(1,128)}, f32[1,224]{1,0:T(1,128)S(1)}, u32[]{:S(2)}, u32[]{:S(2)}) %collective-permute-start.4) | collective-permute-done | bytes 928 | tf_op jit(solution)/shard_map/ppermute | solution.py:21
  6.8 3.5 %collective-permute-start.2 = (bf16[4,3584]{1,0:T(4,128)(2,1)}, bf16[4,3584]{1,0:T(4,128)(2,1)S(1)}, u32[]{:S(2)}, u32[]{:S(2)}) collective-permute-start(bf16[4,3584]{1,0:T(4,128)(2,1)} %resid_hbm.1), channel_id=1, source_target_pairs={{0,7},{1,6},{2,5},{3,4},{4,3},{5,2},{6,1},{7,0},{8,15},{9,14},{10,... | collective-permute-start | bytes 86024 | tf_op jit(solution)/shard_map/ppermute | solution.py:21
  10.3 1.9 %shard_map.92 = (bf16[224,3584]{1,0:T(8,128)(2,1)S(1)}, bf16[224,3584]{1,0:T(8,128)(2,1)S(1)}, f32[1,224]{1,0:T(1,128)S(1)}, bf16[4,3584]{1,0:T(4,128)(2,1)S(1)}) custom-call(bf16[224,3584]{1,0:T(8,128)(2,1)} %dec_hbm.1, bf16[224,3584]{1,0:T(8,128)(2,1)} %enc_hbm.1, f32[1,224]{1,0:T(1,128)} %bitcast.11, bf16[4,3584]{1,0:T(4,128)(2,1)} %resid_hbm.1), custom_call_target="tpu_custom_call" | custom-call | tf_op jit(solution)/shard_map/pallas_call | solution.py:260
  12.3 0.0 collective-permute-done.refs_1_
  12.3 0.0 collective-permute-done.1.refs_2_
  12.3 0.0 collective-permute-done.2.refs_3_
  12.3 0.0 collective-permute-done.5.refs_9_.dec2_ref
  12.3 0.0 collective-permute-done.3.refs_5_
  12.3 1.5 %shard_map.93 = (f32[4,3584]{1,0:T(4,128)S(1)}, f32[4,3584]{1,0:T(4,128)S(1)}, f32[4,3584]{1,0:T(4,128)S(1)}, f32[4,3584]{1,0:T(4,128)S(1)}, bf16[16,224]{1,0:T(8,128)(2,1)S(1)}, /*index=5*/bf16[16,224]{1,0:T(8,128)(2,1)S(1)}) custom-call(bf16[4,3584]{1,0:T(4,128)(2,1)S(1)} %get-tuple-element.25.refs_0_.refs_5_, ...), custom_call_target="tpu_custom_call" | custom-call | tf_op jit(solution)/shard_map/pallas_call | solution.py:250
  13.8 1.5 %collective-permute-start.6 = (f32[4,3584]{1,0:T(4,128)S(1)}, f32[4,3584]{1,0:T(4,128)S(1)}, u32[]{:S(2)}, u32[]{:S(2)}) collective-permute-start(f32[4,3584]{1,0:T(4,128)S(1)} %get-tuple-element.30), channel_id=1, source_target_pairs={{0,3},{1,2},{2,1},{3,0},{4,7},{5,6},{6,5},{7,4},{8,11},{9,10},{10,... | collective-permute-start | bytes 172040 | tf_op jit(solution)/shard_map/ppermute | solution.py:21
  15.3 1.5 %collective-permute-start.7 = (f32[4,3584]{1,0:T(4,128)S(1)}, f32[4,3584]{1,0:T(4,128)S(1)}, u32[]{:S(2)}, u32[]{:S(2)}) collective-permute-start(f32[4,3584]{1,0:T(4,128)S(1)} %get-tuple-element.31), channel_id=1, source_target_pairs={{0,5},{1,4},{2,7},{3,6},{4,1},{5,0},{6,3},{7,2},{8,13},{9,12},{10,... | collective-permute-start | bytes 172040 | tf_op jit(solution)/shard_map/ppermute | solution.py:21
  16.8 0.2 collective-permute-start.8
  17.1 0.0 copy-start
  17.1 0.8 %shard_map.94 = (f32[224,1]{1,0:T(8,128)S(1)}, f32[4,128]{1,0:T(4,128)S(1)}) custom-call(bf16[224,3584]{1,0:T(8,128)(2,1)S(1)} %get-tuple-element.28.refs_8_.dec_ref, bf16[224,3584]{1,0:T(8,128)(2,1)S(1)} %collective-permute-done.5.refs_9_.dec2_ref, bf16[16,224]{1,0:T(8,128)(2,1)S(1)} %get-tuple-element.33.codes_ref, ...), custom_call_target="tpu_custom_call" | custom-call | tf_op jit(solution)/shard_map/pallas_call | solution.py:250
  17.9 0.0 collective-permute-done.6.refs_1_
  17.9 1.1 %collective-permute-done.7.refs_2_ = f32[4,3584]{1,0:T(4,128)S(1)} collective-permute-done((f32[4,3584]{1,0:T(4,128)S(1)}, f32[4,3584]{1,0:T(4,128)S(1)}, u32[]{:S(2)}, u32[]{:S(2)}) %collective-permute-start.7) | collective-permute-done | bytes 57376 | tf_op jit(solution)/shard_map/ppermute | solution.py:21
  19.0 2.6 %collective-permute-done.8.refs_3_ = f32[4,3584]{1,0:T(4,128)S(1)} collective-permute-done((f32[4,3584]{1,0:T(4,128)S(1)}, f32[4,3584]{1,0:T(4,128)S(1)}, u32[]{:S(2)}, u32[]{:S(2)}) %collective-permute-start.8) | collective-permute-done | bytes 57376 | tf_op jit(solution)/shard_map/ppermute | solution.py:21
  21.6 2.6 %collective-permute-start.10 = (f32[4,3712]{1,0:T(4,128)S(1)}, f32[4,3712]{1,0:T(4,128)S(1)}, u32[]{:S(2)}, u32[]{:S(2)}) collective-permute-start(f32[4,3712]{1,0:T(4,128)S(1)} %shard_map.95.refs_0_), channel_id=1, source_target_pairs={{0,16},{8,24},{16,0},{24,8},{1,17},{9,25},{17,1},{25,9},{2,18},{10... | collective-permute-start | bytes 178184 | tf_op jit(solution)/shard_map/ppermute | solution.py:21
  24.3 1.3 %collective-permute-start.11 = (f32[4,3712]{1,0:T(4,128)S(1)}, f32[4,3712]{1,0:T(4,128)S(1)}, u32[]{:S(2)}, u32[]{:S(2)}) collective-permute-start(f32[4,3712]{1,0:T(4,128)S(1)} %shard_map.95.refs_0_), channel_id=1, source_target_pairs={{0,24},{8,16},{16,8},{24,0},{1,25},{9,17},{17,9},{25,1},{2,26},{10... | collective-permute-start | bytes 178184 | tf_op jit(solution)/shard_map/ppermute | solution.py:21
  25.6 0.2 collective-permute-start.9
  25.9 0.0 copy-done
  25.9 2.5 %collective-permute-done.10.refs_2_ = f32[4,3712]{1,0:T(4,128)S(1)} collective-permute-done((f32[4,3712]{1,0:T(4,128)S(1)}, f32[4,3712]{1,0:T(4,128)S(1)}, u32[]{:S(2)}, u32[]{:S(2)}) %collective-permute-start.10) | collective-permute-done | bytes 59424 | tf_op jit(solution)/shard_map/ppermute | solution.py:21
  28.3 2.1 %collective-permute-done.11.refs_3_ = f32[4,3712]{1,0:T(4,128)S(1)} collective-permute-done((f32[4,3712]{1,0:T(4,128)S(1)}, f32[4,3712]{1,0:T(4,128)S(1)}, u32[]{:S(2)}, u32[]{:S(2)}) %collective-permute-start.11) | collective-permute-done | bytes 59424 | tf_op jit(solution)/shard_map/ppermute | solution.py:21
  30.4 0.2 collective-permute-done.9.refs_1_
  30.6 0.1 shard_map.97
  30.7 0.1 collective-permute-start.12
  30.8 0.6 %collective-permute-start.13 = (bf16[8,2816]{1,0:T(8,128)(2,1)S(1)}, bf16[8,2816]{1,0:T(8,128)(2,1)S(1)}, u32[]{:S(2)}, u32[]{:S(2)}) collective-permute-start(bf16[8,2816]{1,0:T(8,128)(2,1)S(1)} %shard_map.97), channel_id=1, source_target_pairs={{0,5},{1,4},{2,7},{3,6},{4,1},{5,0},{6,3},{7,2},{8,13},{9,12},{10,... | collective-permute-start | bytes 135176 | tf_op jit(solution)/shard_map/ppermute | solution.py:21
  31.4 1.2 %collective-permute-start.14 = (bf16[8,2816]{1,0:T(8,128)(2,1)S(1)}, bf16[8,2816]{1,0:T(8,128)(2,1)S(1)}, u32[]{:S(2)}, u32[]{:S(2)}) collective-permute-start(bf16[8,2816]{1,0:T(8,128)(2,1)S(1)} %shard_map.97), channel_id=1, source_target_pairs={{0,7},{1,6},{2,5},{3,4},{4,3},{5,2},{6,1},{7,0},{8,15},{9,14},{10,... | collective-permute-start | bytes 135176 | tf_op jit(solution)/shard_map/ppermute | solution.py:21
  32.6 1.7 %collective-permute-done.12 = bf16[8,2816]{1,0:T(8,128)(2,1)S(1)} collective-permute-done((bf16[8,2816]{1,0:T(8,128)(2,1)S(1)}, bf16[8,2816]{1,0:T(8,128)(2,1)S(1)}, u32[]{:S(2)}, u32[]{:S(2)}) %collective-permute-start.12) | collective-permute-done | bytes 45088 | tf_op jit(solution)/shard_map/ppermute | solution.py:21
  34.3 0.1 collective-permute-done.13
  34.4 1.6 %collective-permute-done.14 = bf16[8,2816]{1,0:T(8,128)(2,1)S(1)} collective-permute-done((bf16[8,2816]{1,0:T(8,128)(2,1)S(1)}, bf16[8,2816]{1,0:T(8,128)(2,1)S(1)}, u32[]{:S(2)}, u32[]{:S(2)}) %collective-permute-start.14) | collective-permute-done | bytes 45088 | tf_op jit(solution)/shard_map/ppermute | solution.py:21
  36.0 0.2 collective-permute-start.15
  36.2 0.4 collective-permute-start.16
  36.6 0.9 %collective-permute-done.16.others_ref = bf16[16,224]{1,0:T(8,128)(2,1)S(1)} collective-permute-done((bf16[16,224]{1,0:T(8,128)(2,1)S(1)}, bf16[16,224]{1,0:T(8,128)(2,1)S(1)}, u32[]{:S(2)}, u32[]{:S(2)}) %collective-permute-start.16) | collective-permute-done | bytes 7200 | tf_op jit(solution)/shard_map/ppermute | solution.py:21
  37.5 0.8 %shard_map.98 = (bf16[224,32]{1,0:T(8,128)(2,1)S(1)}, f32[224,1]{1,0:T(8,128)S(1)}, bf16[3584,224]{1,0:T(8,128)(2,1)S(1)}, f32[1,224]{1,0:T(1,128)S(1)}) custom-call(bf16[16,224]{1,0:T(8,128)(2,1)S(1)} %get-tuple-element.33.codes_ref, bf16[16,224]{1,0:T(8,128)(2,1)S(1)} %collective-permute-done.16.others_ref, ...), custom_call_target="tpu_custom_call" | custom-call | tf_op jit(solution)/shard_map/pallas_call | solution.py:250
  38.3 0.6 %shard_map.96 = f32[4,3584]{1,0:T(4,128)} custom-call(f32[4,3712]{1,0:T(4,128)S(1)} %shard_map.95.refs_0_, f32[4,3712]{1,0:T(4,128)S(1)} %collective-permute-done.9.refs_1_, f32[4,3712]{1,0:T(4,128)S(1)} %collective-permute-done.10.refs_2_, f32[4,3712]{1,0:T(4,128)S(1)} %collective-permute-done.11.refs_3_, f32[1,3584]{1,0:T(1,128)S(1)} %reshape.20.refs_4_), custom_call_target="tpu_custom_call" | custom-call | tf_op jit(solution)/shard_map/pallas_call | solution.py:304
  39.0 0.0 collective-permute-done.15.other_ref
  39.0 1.7 %shard_map.99 = (bf16[224,3584]{1,0:T(8,128)(2,1)}, f32[32,224]{1,0:T(8,128)}, f32[3584]{0:T(1024)}, f32[1,1]{1,0:T(1,128)}) custom-call(bf16[4,8,2816]{2,1,0:T(8,128)(2,1)S(1)} %pad_maximum_fusion.near_ref, bf16[4,8,2816]{2,1,0:T(8,128)(2,1)S(1)} %collective-permute-done.15.other_ref, bf16[224,32]{1,0:T(8,128)(2,1)S(1)} %get-tuple-element.37.codes_ref, ...), custom_call_target="tpu_custom_call" | custom-call | tf_op jit(solution)/shard_map/pallas_call | solution.py:315
  (3 shorter events, 0.1 us)
Async XLA Ops:
  0.6 11.7 %collective-permute-start.5 = (bf16[224,3584]{1,0:T(8,128)(2,1)}, bf16[224,3584]{1,0:T(8,128)(2,1)S(1)}, u32[]{:S(2)}, u32[]{:S(2)}) collective-permute-start(bf16[224,3584]{1,0:T(8,128)(2,1)} %dec_hbm.1), channel_id=1, source_target_pairs={{0,1},{1,0},{2,3},{3,2},{4,5},{5,4},{6,7},{7,6},{8,9},{9,8},{10,11... | collective-permute-start | bytes 4816904 | tf_op jit(solution)/shard_map/ppermute | solution.py:21
  1.2 11.1 %collective-permute-start.3 = (bf16[224,3584]{1,0:T(8,128)(2,1)}, bf16[224,3584]{1,0:T(8,128)(2,1)S(1)}, u32[]{:S(2)}, u32[]{:S(2)}) collective-permute-start(bf16[224,3584]{1,0:T(8,128)(2,1)} %enc_hbm.1), channel_id=1, source_target_pairs={{0,1},{1,0},{2,3},{3,2},{4,5},{5,4},{6,7},{7,6},{8,9},{9,8},{10,11... | collective-permute-start | bytes 4816904 | tf_op jit(solution)/shard_map/ppermute | solution.py:21
  1.3 5.5 %collective-permute-start.4 = (f32[1,224]{1,0:T(1,128)}, f32[1,224]{1,0:T(1,128)S(1)}, u32[]{:S(2)}, u32[]{:S(2)}) collective-permute-start(f32[1,224]{1,0:T(1,128)} %bitcast.10), channel_id=1, source_target_pairs={{0,1},{1,0},{2,3},{3,2},{4,5},{5,4},{6,7},{7,6},{8,9},{9,8},{10,11... | collective-permute-start | bytes 2696 | tf_op jit(solution)/shard_map/ppermute | solution.py:21
  1.7 10.6 %collective-permute-start = (bf16[4,3584]{1,0:T(4,128)(2,1)}, bf16[4,3584]{1,0:T(4,128)(2,1)S(1)}, u32[]{:S(2)}, u32[]{:S(2)}) collective-permute-start(bf16[4,3584]{1,0:T(4,128)(2,1)} %resid_hbm.1), channel_id=1, source_target_pairs={{0,3},{1,2},{2,1},{3,0},{4,7},{5,6},{6,5},{7,4},{8,11},{9,10},{10,... | collective-permute-start | bytes 86024 | tf_op jit(solution)/shard_map/ppermute | solution.py:21
  4.3 8.0 %collective-permute-start.1 = (bf16[4,3584]{1,0:T(4,128)(2,1)}, bf16[4,3584]{1,0:T(4,128)(2,1)S(1)}, u32[]{:S(2)}, u32[]{:S(2)}) collective-permute-start(bf16[4,3584]{1,0:T(4,128)(2,1)} %resid_hbm.1), channel_id=1, source_target_pairs={{0,5},{1,4},{2,7},{3,6},{4,1},{5,0},{6,3},{7,2},{8,13},{9,12},{10,... | collective-permute-start | bytes 86024 | tf_op jit(solution)/shard_map/ppermute | solution.py:21
  6.8 5.5 %collective-permute-start.2 = (bf16[4,3584]{1,0:T(4,128)(2,1)}, bf16[4,3584]{1,0:T(4,128)(2,1)S(1)}, u32[]{:S(2)}, u32[]{:S(2)}) collective-permute-start(bf16[4,3584]{1,0:T(4,128)(2,1)} %resid_hbm.1), channel_id=1, source_target_pairs={{0,7},{1,6},{2,5},{3,4},{4,3},{5,2},{6,1},{7,0},{8,15},{9,14},{10,... | collective-permute-start | bytes 86024 | tf_op jit(solution)/shard_map/ppermute | solution.py:21
  13.8 4.0 %collective-permute-start.6 = (f32[4,3584]{1,0:T(4,128)S(1)}, f32[4,3584]{1,0:T(4,128)S(1)}, u32[]{:S(2)}, u32[]{:S(2)}) collective-permute-start(f32[4,3584]{1,0:T(4,128)S(1)} %get-tuple-element.30), channel_id=1, source_target_pairs={{0,3},{1,2},{2,1},{3,0},{4,7},{5,6},{6,5},{7,4},{8,11},{9,10},{10,... | collective-permute-start | bytes 172040 | tf_op jit(solution)/shard_map/ppermute | solution.py:21
  15.3 3.7 %collective-permute-start.7 = (f32[4,3584]{1,0:T(4,128)S(1)}, f32[4,3584]{1,0:T(4,128)S(1)}, u32[]{:S(2)}, u32[]{:S(2)}) collective-permute-start(f32[4,3584]{1,0:T(4,128)S(1)} %get-tuple-element.31), channel_id=1, source_target_pairs={{0,5},{1,4},{2,7},{3,6},{4,1},{5,0},{6,3},{7,2},{8,13},{9,12},{10,... | collective-permute-start | bytes 172040 | tf_op jit(solution)/shard_map/ppermute | solution.py:21
  16.8 4.8 %collective-permute-start.8 = (f32[4,3584]{1,0:T(4,128)S(1)}, f32[4,3584]{1,0:T(4,128)S(1)}, u32[]{:S(2)}, u32[]{:S(2)}) collective-permute-start(f32[4,3584]{1,0:T(4,128)S(1)} %get-tuple-element.32), channel_id=1, source_target_pairs={{0,7},{1,6},{2,5},{3,4},{4,3},{5,2},{6,1},{7,0},{8,15},{9,14},{10,... | collective-permute-start | bytes 172040 | tf_op jit(solution)/shard_map/ppermute | solution.py:21
  17.1 8.8 %copy-start = (f32[3584]{0:T(1024)S(1)}, f32[3584]{0:T(1024)}, u32[]{:S(2)}) copy-start(f32[3584]{0:T(1024)} %param.9) | copy-start | bytes 43012
  21.6 6.7 %collective-permute-start.10 = (f32[4,3712]{1,0:T(4,128)S(1)}, f32[4,3712]{1,0:T(4,128)S(1)}, u32[]{:S(2)}, u32[]{:S(2)}) collective-permute-start(f32[4,3712]{1,0:T(4,128)S(1)} %shard_map.95.refs_0_), channel_id=1, source_target_pairs={{0,16},{8,24},{16,0},{24,8},{1,17},{9,25},{17,1},{25,9},{2,18},{10... | collective-permute-start | bytes 178184 | tf_op jit(solution)/shard_map/ppermute | solution.py:21
  24.3 6.2 %collective-permute-start.11 = (f32[4,3712]{1,0:T(4,128)S(1)}, f32[4,3712]{1,0:T(4,128)S(1)}, u32[]{:S(2)}, u32[]{:S(2)}) collective-permute-start(f32[4,3712]{1,0:T(4,128)S(1)} %shard_map.95.refs_0_), channel_id=1, source_target_pairs={{0,24},{8,16},{16,8},{24,0},{1,25},{9,17},{17,9},{25,1},{2,26},{10... | collective-permute-start | bytes 178184 | tf_op jit(solution)/shard_map/ppermute | solution.py:21
  25.6 5.0 %collective-permute-start.9 = (f32[4,3712]{1,0:T(4,128)S(1)}, f32[4,3712]{1,0:T(4,128)S(1)}, u32[]{:S(2)}, u32[]{:S(2)}) collective-permute-start(f32[4,3712]{1,0:T(4,128)S(1)} %shard_map.95.refs_0_), channel_id=1, source_target_pairs={{0,8},{8,0},{16,24},{24,16},{1,9},{9,1},{17,25},{25,17},{2,10},{10... | collective-permute-start | bytes 178184 | tf_op jit(solution)/shard_map/ppermute | solution.py:21
  30.7 3.5 %collective-permute-start.12 = (bf16[8,2816]{1,0:T(8,128)(2,1)S(1)}, bf16[8,2816]{1,0:T(8,128)(2,1)S(1)}, u32[]{:S(2)}, u32[]{:S(2)}) collective-permute-start(bf16[8,2816]{1,0:T(8,128)(2,1)S(1)} %shard_map.97), channel_id=1, source_target_pairs={{0,3},{1,2},{2,1},{3,0},{4,7},{5,6},{6,5},{7,4},{8,11},{9,10},{10,... | collective-permute-start | bytes 135176 | tf_op jit(solution)/shard_map/ppermute | solution.py:21
  30.8 3.5 %collective-permute-start.13 = (bf16[8,2816]{1,0:T(8,128)(2,1)S(1)}, bf16[8,2816]{1,0:T(8,128)(2,1)S(1)}, u32[]{:S(2)}, u32[]{:S(2)}) collective-permute-start(bf16[8,2816]{1,0:T(8,128)(2,1)S(1)} %shard_map.97), channel_id=1, source_target_pairs={{0,5},{1,4},{2,7},{3,6},{4,1},{5,0},{6,3},{7,2},{8,13},{9,12},{10,... | collective-permute-start | bytes 135176 | tf_op jit(solution)/shard_map/ppermute | solution.py:21
  31.4 4.6 %collective-permute-start.14 = (bf16[8,2816]{1,0:T(8,128)(2,1)S(1)}, bf16[8,2816]{1,0:T(8,128)(2,1)S(1)}, u32[]{:S(2)}, u32[]{:S(2)}) collective-permute-start(bf16[8,2816]{1,0:T(8,128)(2,1)S(1)} %shard_map.97), channel_id=1, source_target_pairs={{0,7},{1,6},{2,5},{3,4},{4,3},{5,2},{6,1},{7,0},{8,15},{9,14},{10,... | collective-permute-start | bytes 135176 | tf_op jit(solution)/shard_map/ppermute | solution.py:21
  36.0 3.0 %collective-permute-start.15 = (bf16[4,8,2816]{2,1,0:T(8,128)(2,1)S(1)}, bf16[4,8,2816]{2,1,0:T(8,128)(2,1)S(1)}, u32[]{:S(2)}, u32[]{:S(2)}) collective-permute-start(bf16[4,8,2816]{2,1,0:T(8,128)(2,1)S(1)} %pad_maximum_fusion.near_ref), channel_id=1, source_target_pairs={{0,1},{1,0},{2,3},{3,2},{4,5},{5,4},{6,7},{7,6},{8,9},{9,8},{10,11... | collective-permute-start | bytes 540680 | tf_op jit(solution)/shard_map/ppermute | solution.py:21
  36.2 1.3 %collective-permute-start.16 = (bf16[16,224]{1,0:T(8,128)(2,1)S(1)}, bf16[16,224]{1,0:T(8,128)(2,1)S(1)}, u32[]{:S(2)}, u32[]{:S(2)}) collective-permute-start(bf16[16,224]{1,0:T(8,128)(2,1)S(1)} %get-tuple-element.34.codes2_ref), channel_id=1, source_target_pairs={{0,1},{1,0},{2,3},{3,2},{4,5},{5,4},{6,7},{7,6},{8,9},{9,8},{10,11... | collective-permute-start | bytes 21512 | tf_op jit(solution)/shard_map/ppermute | solution.py:21

commit v4 on v3

--- a/solution.py
+++ b/solution.py
@@ -159,16 +159,14 @@
     out_ref[...] = pack[...].astype(BF16)
 
 
-def backward_kernel(
-    order, near_ref, other_ref, codes_ref, scale_ref, dec_ref, turned_ref, norm_ref,
-    grad_ref, code_grad_ref, column_ref, loss_ref,
-    errors_ref, staged, by_row_ref, column_buf, loss_buf, sems, small_sems,
-):
-    half, rows2, _ = near_ref.shape
-    rows = rows2 // 2
+def backward_kernel(order, *refs):
+    blocks, refs = refs[: len(order)], refs[len(order) :]
+    codes_ref, scale_ref, dec_ref, turned_ref, norm_ref = refs[:5]
+    grad_ref, code_grad_ref, column_ref, loss_ref = refs[5:9]
+    errors_ref, staged, by_row_ref, column_buf, loss_buf, sems, small_sems = refs[9:]
+    half, rows = len(order) // 2, blocks[0].shape[0] // 2
     lat, width = dec_ref.shape
     cut, piece = width // 2, width // rows
-    blocks = [near_ref.at[p] if p < half else other_ref.at[p - half] for p in range(2 * half)]
     codes, scale = codes_ref[...], scale_ref[...]
     n_chunks, _, chunk = staged.shape
     copies = []
@@ -192,7 +190,7 @@
         write_grad(i)
 
     by_row = jnp.broadcast_to(norm_ref[...], (2 * half * rows, lat))
-    step = chunk_of(width)
+    step = width // 2
     for c in range(0, width, step):
         by_row = by_row + contract(errors_ref[:, c : c + step], turned_ref[c : c + step], ((1,), (0,)))
     me = lax.axis_index("tensor")
@@ -300,7 +298,7 @@
         compiler_params=PARAMS,
         scratch_shapes=[pltpu.VMEM((2 * rows, packed), F32)],
     )(*terms, bias, own)
-    near = jnp.stack([payload] + swaps([payload] * half, "tensor", n_tensor, masks[1:]))
+    near = [payload] + swaps([payload] * half, "tensor", n_tensor, masks[1:])
     recon = pl.pallas_call(
         functools.partial(recon_kernel, len(terms)),
         out_shape=shape((rows, width), F32),
@@ -308,7 +306,7 @@
         out_specs=VMEM,
         compiler_params=PARAMS,
     )(*terms, bias)
-    other = swap(near, "tensor", n_tensor, 1)
+    other = [mate(x) for x in near]
     chunk = width // 4
     n_chunks = width // chunk
     by_row = (total_rows, lat) if rows % 4 == 0 else (n_tensor, rows, lat)
@@ -320,7 +318,7 @@
             shape((width,), F32),
             shape((1, 1), F32),
         ),
-        in_specs=[VMEM] * 7,
+        in_specs=[VMEM] * (2 * half + 5),
         out_specs=(anywhere,) * 4,
         compiler_params=PARAMS,
         scratch_shapes=[
@@ -332,7 +330,7 @@
             pltpu.SemaphoreType.DMA((n_chunks,)),
             pltpu.SemaphoreType.DMA((3,)),
         ],
-    )(near, other, by_lat, scale, w_dec, turned, norm)
+    )(*near, *other, by_lat, scale, w_dec, turned, norm)
     return recon, grad_w_dec, code_grad.reshape(total_rows, lat), column, loss.reshape(())
 
 

time: 40.8 us -> 40.6 us (level)
  waiting for transfers between devices: 14.1 us -> 11.9 us
  starting transfers between devices: 18.2 us -> 20.3 us
    ppermute x17 -> x20, waiting for transfers between devices: 14.1 us -> 11.9 us  [swap(): return lax.ppermute(x, axis, [(i, i ^ mask) for i in range(size)])]
    ppermute x17 -> x20, starting transfers between devices: 18.2 us -> 20.3 us  [swap(): return lax.ppermute(x, axis, [(i, i ^ mask) for i in range(size)])]
  transfers between devices with their start and end apart: 17 -> 20, of which waited for: 10 -> 10; matrix products, arithmetic and copies ran while one was open for 0% -> 0% of each run, Pallas kernels for 10% -> 10%
where the time goes in v4:
time: 40.6 us; the launch traced here: 40.5 us
  starting transfers between devices  20.3 us (50%)
  waiting for transfers between devices  11.9 us (29%)
  Pallas kernels  7.5 us (18%)
  between operations  0.73 us (2%)
    ppermute x20, starting transfers between devices, swap(): return lax.ppermute(x, axis, [(i, i ^ mask) for i in range(size)])  20.3 us
    ppermute x20, waiting for transfers between devices, swap(): return lax.ppermute(x, axis, [(i, i ^ mask) for i in range(size)])  11.9 us
    pallas_call x4, Pallas kernels, call(): pl.pallas_call(kernel, out_shape=tuple(outs), in_specs=[VMEM] * len(args)...  3.15 us
    pallas_call x1, Pallas kernels, per_device(): pl.pallas_call(fetch_kernel, out_shape=tuple((shape(x.shape, x.dtype) for...  1.94 us
    pallas_call x1, Pallas kernels, per_device(): pl.pallas_call(functools.partial(backward_kernel, order), out_shape=(shap...  1.65 us
  transfers between devices with their start and end apart: 20, of which 10 were waited for; matrix products, arithmetic and copies ran while one was open for 0% of the time, Pallas kernels for 10%

profile of v4, /device:TPU:0, one launch (start us, length us, event | category | flops | bytes accessed | tf_op | source)
XLA Modules:
  0.0 40.5 jit_solution(13503344539761643238)
XLA Ops:
  0.6 0.6 %collective-permute-start.5 = (bf16[224,3584]{1,0:T(8,128)(2,1)}, bf16[224,3584]{1,0:T(8,128)(2,1)S(1)}, u32[]{:S(2)}, u32[]{:S(2)}) collective-permute-start(bf16[224,3584]{1,0:T(8,128)(2,1)} %dec_hbm.1), channel_id=1, source_target_pairs={{0,1},{1,0},{2,3},{3,2},{4,5},{5,4},{6,7},{7,6},{8,9},{9,8},{10,11... | collective-permute-start | bytes 4816904 | tf_op jit(solution)/shard_map/ppermute | solution.py:21
  1.2 0.1 collective-permute-start.3
  1.3 0.4 %collective-permute-start.4 = (f32[1,224]{1,0:T(1,128)}, f32[1,224]{1,0:T(1,128)S(1)}, u32[]{:S(2)}, u32[]{:S(2)}) collective-permute-start(f32[1,224]{1,0:T(1,128)} %bitcast.2), channel_id=1, source_target_pairs={{0,1},{1,0},{2,3},{3,2},{4,5},{5,4},{6,7},{7,6},{8,9},{9,8},{10,11... | collective-permute-start | bytes 2696 | tf_op jit(solution)/shard_map/ppermute | solution.py:21
  1.7 2.6 %collective-permute-start = (bf16[4,3584]{1,0:T(4,128)(2,1)}, bf16[4,3584]{1,0:T(4,128)(2,1)S(1)}, u32[]{:S(2)}, u32[]{:S(2)}) collective-permute-start(bf16[4,3584]{1,0:T(4,128)(2,1)} %resid_hbm.1), channel_id=1, source_target_pairs={{0,3},{1,2},{2,1},{3,0},{4,7},{5,6},{6,5},{7,4},{8,11},{9,10},{10,... | collective-permute-start | bytes 86024 | tf_op jit(solution)/shard_map/ppermute | solution.py:21
  4.3 1.2 %collective-permute-start.1 = (bf16[4,3584]{1,0:T(4,128)(2,1)}, bf16[4,3584]{1,0:T(4,128)(2,1)S(1)}, u32[]{:S(2)}, u32[]{:S(2)}) collective-permute-start(bf16[4,3584]{1,0:T(4,128)(2,1)} %resid_hbm.1), channel_id=1, source_target_pairs={{0,5},{1,4},{2,7},{3,6},{4,1},{5,0},{6,3},{7,2},{8,13},{9,12},{10,... | collective-permute-start | bytes 86024 | tf_op jit(solution)/shard_map/ppermute | solution.py:21
  5.5 1.3 %collective-permute-done.4.refs_7_ = f32[1,224]{1,0:T(1,128)S(1)} collective-permute-done((f32[1,224]{1,0:T(1,128)}, f32[1,224]{1,0:T(1,128)S(1)}, u32[]{:S(2)}, u32[]{:S(2)}) %collective-permute-start.4) | collective-permute-done | bytes 928 | tf_op jit(solution)/shard_map/ppermute | solution.py:21
  6.8 3.5 %collective-permute-start.2 = (bf16[4,3584]{1,0:T(4,128)(2,1)}, bf16[4,3584]{1,0:T(4,128)(2,1)S(1)}, u32[]{:S(2)}, u32[]{:S(2)}) collective-permute-start(bf16[4,3584]{1,0:T(4,128)(2,1)} %resid_hbm.1), channel_id=1, source_target_pairs={{0,7},{1,6},{2,5},{3,4},{4,3},{5,2},{6,1},{7,0},{8,15},{9,14},{10,... | collective-permute-start | bytes 86024 | tf_op jit(solution)/shard_map/ppermute | solution.py:21
  10.3 1.9 %shard_map.92 = (bf16[224,3584]{1,0:T(8,128)(2,1)S(1)}, bf16[224,3584]{1,0:T(8,128)(2,1)S(1)}, f32[1,224]{1,0:T(1,128)S(1)}, bf16[4,3584]{1,0:T(4,128)(2,1)S(1)}) custom-call(bf16[224,3584]{1,0:T(8,128)(2,1)} %dec_hbm.1, bf16[224,3584]{1,0:T(8,128)(2,1)} %enc_hbm.1, f32[1,224]{1,0:T(1,128)} %bitcast.3, bf16[4,3584]{1,0:T(4,128)(2,1)} %resid_hbm.1), custom_call_target="tpu_custom_call" | custom-call | tf_op jit(solution)/shard_map/pallas_call | solution.py:258
  12.3 0.0 collective-permute-done.refs_1_
  12.3 0.0 collective-permute-done.1.refs_2_
  12.3 0.0 collective-permute-done.2.refs_3_
  12.3 0.0 collective-permute-done.5.refs_9_.dec2_ref
  12.3 0.0 collective-permute-done.3.refs_5_
  12.3 1.5 %shard_map.93 = (f32[4,3584]{1,0:T(4,128)S(1)}, f32[4,3584]{1,0:T(4,128)S(1)}, f32[4,3584]{1,0:T(4,128)S(1)}, f32[4,3584]{1,0:T(4,128)S(1)}, bf16[16,224]{1,0:T(8,128)(2,1)S(1)}, /*index=5*/bf16[16,224]{1,0:T(8,128)(2,1)S(1)}) custom-call(bf16[4,3584]{1,0:T(4,128)(2,1)S(1)} %get-tuple-element.25.refs_0_.refs_5_, ...), custom_call_target="tpu_custom_call" | custom-call | tf_op jit(solution)/shard_map/pallas_call | solution.py:248
  13.8 1.5 %collective-permute-start.6 = (f32[4,3584]{1,0:T(4,128)S(1)}, f32[4,3584]{1,0:T(4,128)S(1)}, u32[]{:S(2)}, u32[]{:S(2)}) collective-permute-start(f32[4,3584]{1,0:T(4,128)S(1)} %get-tuple-element.30), channel_id=1, source_target_pairs={{0,3},{1,2},{2,1},{3,0},{4,7},{5,6},{6,5},{7,4},{8,11},{9,10},{10,... | collective-permute-start | bytes 172040 | tf_op jit(solution)/shard_map/ppermute | solution.py:21
  15.3 1.5 %collective-permute-start.7 = (f32[4,3584]{1,0:T(4,128)S(1)}, f32[4,3584]{1,0:T(4,128)S(1)}, u32[]{:S(2)}, u32[]{:S(2)}) collective-permute-start(f32[4,3584]{1,0:T(4,128)S(1)} %get-tuple-element.31), channel_id=1, source_target_pairs={{0,5},{1,4},{2,7},{3,6},{4,1},{5,0},{6,3},{7,2},{8,13},{9,12},{10,... | collective-permute-start | bytes 172040 | tf_op jit(solution)/shard_map/ppermute | solution.py:21
  16.8 0.2 collective-permute-start.8
  17.1 0.0 copy-start
  17.1 0.8 %shard_map.94 = (f32[224,1]{1,0:T(8,128)S(1)}, f32[4,128]{1,0:T(4,128)S(1)}) custom-call(bf16[224,3584]{1,0:T(8,128)(2,1)S(1)} %get-tuple-element.28.refs_8_.dec_ref.refs_10_, bf16[224,3584]{1,0:T(8,128)(2,1)S(1)} %collective-permute-done.5.refs_9_.dec2_ref, bf16[16,224]{1,0:T(8,128)(2,1)S(1)} %get-tuple-element.33.codes_ref, ...), custom_call_target="tpu_custom_call" | custom-call | tf_op jit(solution)/shard_map/pallas_call | solution.py:248
  17.9 0.0 collective-permute-done.6.refs_1_
  17.9 1.1 %collective-permute-done.7.refs_2_ = f32[4,3584]{1,0:T(4,128)S(1)} collective-permute-done((f32[4,3584]{1,0:T(4,128)S(1)}, f32[4,3584]{1,0:T(4,128)S(1)}, u32[]{:S(2)}, u32[]{:S(2)}) %collective-permute-start.7) | collective-permute-done | bytes 57376 | tf_op jit(solution)/shard_map/ppermute | solution.py:21
  19.0 2.6 %collective-permute-done.8.refs_3_ = f32[4,3584]{1,0:T(4,128)S(1)} collective-permute-done((f32[4,3584]{1,0:T(4,128)S(1)}, f32[4,3584]{1,0:T(4,128)S(1)}, u32[]{:S(2)}, u32[]{:S(2)}) %collective-permute-start.8) | collective-permute-done | bytes 57376 | tf_op jit(solution)/shard_map/ppermute | solution.py:21
  21.6 2.6 %collective-permute-start.10 = (f32[4,3712]{1,0:T(4,128)S(1)}, f32[4,3712]{1,0:T(4,128)S(1)}, u32[]{:S(2)}, u32[]{:S(2)}) collective-permute-start(f32[4,3712]{1,0:T(4,128)S(1)} %shard_map.95.refs_0_), channel_id=1, source_target_pairs={{0,16},{8,24},{16,0},{24,8},{1,17},{9,25},{17,1},{25,9},{2,18},{10... | collective-permute-start | bytes 178184 | tf_op jit(solution)/shard_map/ppermute | solution.py:21
  24.3 1.3 %collective-permute-start.11 = (f32[4,3712]{1,0:T(4,128)S(1)}, f32[4,3712]{1,0:T(4,128)S(1)}, u32[]{:S(2)}, u32[]{:S(2)}) collective-permute-start(f32[4,3712]{1,0:T(4,128)S(1)} %shard_map.95.refs_0_), channel_id=1, source_target_pairs={{0,24},{8,16},{16,8},{24,0},{1,25},{9,17},{17,9},{25,1},{2,26},{10... | collective-permute-start | bytes 178184 | tf_op jit(solution)/shard_map/ppermute | solution.py:21
  25.6 0.2 collective-permute-start.9
  25.9 0.0 copy-done
  25.9 2.5 %collective-permute-done.10.refs_2_ = f32[4,3712]{1,0:T(4,128)S(1)} collective-permute-done((f32[4,3712]{1,0:T(4,128)S(1)}, f32[4,3712]{1,0:T(4,128)S(1)}, u32[]{:S(2)}, u32[]{:S(2)}) %collective-permute-start.10) | collective-permute-done | bytes 59424 | tf_op jit(solution)/shard_map/ppermute | solution.py:21
  28.3 2.1 %collective-permute-done.11.refs_3_ = f32[4,3712]{1,0:T(4,128)S(1)} collective-permute-done((f32[4,3712]{1,0:T(4,128)S(1)}, f32[4,3712]{1,0:T(4,128)S(1)}, u32[]{:S(2)}, u32[]{:S(2)}) %collective-permute-start.11) | collective-permute-done | bytes 59424 | tf_op jit(solution)/shard_map/ppermute | solution.py:21
  30.4 0.2 collective-permute-done.9.refs_1_
  30.6 0.1 shard_map.97.refs_0_
  30.7 0.1 collective-permute-start.12
  30.8 0.6 %collective-permute-start.13 = (bf16[8,2816]{1,0:T(8,128)(2,1)S(1)}, bf16[8,2816]{1,0:T(8,128)(2,1)S(1)}, u32[]{:S(2)}, u32[]{:S(2)}) collective-permute-start(bf16[8,2816]{1,0:T(8,128)(2,1)S(1)} %shard_map.97.refs_0_), channel_id=1, source_target_pairs={{0,5},{1,4},{2,7},{3,6},{4,1},{5,0},{6,3},{7,2},{8,13},{9,12},{10,... | collective-permute-start | bytes 135176 | tf_op jit(solution)/shard_map/ppermute | solution.py:21
  31.4 1.2 %collective-permute-start.14 = (bf16[8,2816]{1,0:T(8,128)(2,1)S(1)}, bf16[8,2816]{1,0:T(8,128)(2,1)S(1)}, u32[]{:S(2)}, u32[]{:S(2)}) collective-permute-start(bf16[8,2816]{1,0:T(8,128)(2,1)S(1)} %shard_map.97.refs_0_), channel_id=1, source_target_pairs={{0,7},{1,6},{2,5},{3,4},{4,3},{5,2},{6,1},{7,0},{8,15},{9,14},{10,... | collective-permute-start | bytes 135176 | tf_op jit(solution)/shard_map/ppermute | solution.py:21
  32.6 1.5 %collective-permute-start.15 = (bf16[8,2816]{1,0:T(8,128)(2,1)S(1)}, bf16[8,2816]{1,0:T(8,128)(2,1)S(1)}, u32[]{:S(2)}, u32[]{:S(2)}) collective-permute-start(bf16[8,2816]{1,0:T(8,128)(2,1)S(1)} %shard_map.97.refs_0_), channel_id=1, source_target_pairs={{0,1},{1,0},{2,3},{3,2},{4,5},{5,4},{6,7},{7,6},{8,9},{9,8},{10,11... | collective-permute-start | bytes 135176 | tf_op jit(solution)/shard_map/ppermute | solution.py:21
  34.1 0.1 collective-permute-done.12.refs_1_
  34.3 0.0 collective-permute-start.16
  34.3 0.1 collective-permute-done.13.refs_2_
  34.4 0.6 %collective-permute-start.17 = (bf16[8,2816]{1,0:T(8,128)(2,1)S(1)}, bf16[8,2816]{1,0:T(8,128)(2,1)S(1)}, u32[]{:S(2)}, u32[]{:S(2)}) collective-permute-start(bf16[8,2816]{1,0:T(8,128)(2,1)S(1)} %collective-permute-done.13.refs_2_), channel_id=1, source_target_pairs={{0,1},{1,0},{2,3},{3,2},{4,5},{5,4},{6,7},{7,6},{8,9},{9,8},{10,11... | collective-permute-start | bytes 135176 | tf_op jit(solution)/shard_map/ppermute | solution.py:21
  34.9 1.1 %collective-permute-done.14.refs_3_ = bf16[8,2816]{1,0:T(8,128)(2,1)S(1)} collective-permute-done((bf16[8,2816]{1,0:T(8,128)(2,1)S(1)}, bf16[8,2816]{1,0:T(8,128)(2,1)S(1)}, u32[]{:S(2)}, u32[]{:S(2)}) %collective-permute-start.14) | collective-permute-done | bytes 45088 | tf_op jit(solution)/shard_map/ppermute | solution.py:21
  36.0 0.1 collective-permute-start.18
  36.1 0.4 collective-permute-start.19
  36.5 0.8 %collective-permute-done.19.others_ref = bf16[16,224]{1,0:T(8,128)(2,1)S(1)} collective-permute-done((bf16[16,224]{1,0:T(8,128)(2,1)S(1)}, bf16[16,224]{1,0:T(8,128)(2,1)S(1)}, u32[]{:S(2)}, u32[]{:S(2)}) %collective-permute-start.19) | collective-permute-done | bytes 7200 | tf_op jit(solution)/shard_map/ppermute | solution.py:21
  37.3 0.8 %shard_map.98 = (bf16[224,32]{1,0:T(8,128)(2,1)S(1)}, f32[224,1]{1,0:T(8,128)S(1)}, bf16[3584,224]{1,0:T(8,128)(2,1)S(1)}, f32[1,224]{1,0:T(1,128)S(1)}) custom-call(bf16[16,224]{1,0:T(8,128)(2,1)S(1)} %get-tuple-element.33.codes_ref, bf16[16,224]{1,0:T(8,128)(2,1)S(1)} %collective-permute-done.19.others_ref, ...), custom_call_target="tpu_custom_call" | custom-call | tf_op jit(solution)/shard_map/pallas_call | solution.py:248
  38.1 0.6 %shard_map.96 = f32[4,3584]{1,0:T(4,128)} custom-call(f32[4,3712]{1,0:T(4,128)S(1)} %shard_map.95.refs_0_, f32[4,3712]{1,0:T(4,128)S(1)} %collective-permute-done.9.refs_1_, f32[4,3712]{1,0:T(4,128)S(1)} %collective-permute-done.10.refs_2_, f32[4,3712]{1,0:T(4,128)S(1)} %collective-permute-done.11.refs_3_, f32[1,3584]{1,0:T(1,128)S(1)} %reshape.20.refs_4_), custom_call_target="tpu_custom_call" | custom-call | tf_op jit(solution)/shard_map/pallas_call | solution.py:302
  38.8 0.0 collective-permute-done.15.refs_4_
  38.8 0.0 collective-permute-done.16.refs_5_
  38.8 0.0 collective-permute-done.17.refs_6_
  38.8 0.0 collective-permute-done.18.refs_7_
  38.8 1.7 %shard_map.99 = (bf16[224,3584]{1,0:T(8,128)(2,1)}, f32[32,224]{1,0:T(8,128)}, f32[3584]{0:T(1024)}, f32[1,1]{1,0:T(1,128)}) custom-call(bf16[8,2816]{1,0:T(8,128)(2,1)S(1)} %shard_map.97.refs_0_, bf16[8,2816]{1,0:T(8,128)(2,1)S(1)} %collective-permute-done.12.refs_1_, bf16[8,2816]{1,0:T(8,128)(2,1)S(1)} %collective-permute-done.13.refs_2_, ...), custom_call_target="tpu_custom_call" | custom-call | tf_op jit(solution)/shard_map/pallas_call | solution.py:313
  (2 shorter events, 0.0 us)
Async XLA Ops:
  0.6 11.7 %collective-permute-start.5 = (bf16[224,3584]{1,0:T(8,128)(2,1)}, bf16[224,3584]{1,0:T(8,128)(2,1)S(1)}, u32[]{:S(2)}, u32[]{:S(2)}) collective-permute-start(bf16[224,3584]{1,0:T(8,128)(2,1)} %dec_hbm.1), channel_id=1, source_target_pairs={{0,1},{1,0},{2,3},{3,2},{4,5},{5,4},{6,7},{7,6},{8,9},{9,8},{10,11... | collective-permute-start | bytes 4816904 | tf_op jit(solution)/shard_map/ppermute | solution.py:21
  1.2 11.1 %collective-permute-start.3 = (bf16[224,3584]{1,0:T(8,128)(2,1)}, bf16[224,3584]{1,0:T(8,128)(2,1)S(1)}, u32[]{:S(2)}, u32[]{:S(2)}) collective-permute-start(bf16[224,3584]{1,0:T(8,128)(2,1)} %enc_hbm.1), channel_id=1, source_target_pairs={{0,1},{1,0},{2,3},{3,2},{4,5},{5,4},{6,7},{7,6},{8,9},{9,8},{10,11... | collective-permute-start | bytes 4816904 | tf_op jit(solution)/shard_map/ppermute | solution.py:21
  1.3 5.5 %collective-permute-start.4 = (f32[1,224]{1,0:T(1,128)}, f32[1,224]{1,0:T(1,128)S(1)}, u32[]{:S(2)}, u32[]{:S(2)}) collective-permute-start(f32[1,224]{1,0:T(1,128)} %bitcast.2), channel_id=1, source_target_pairs={{0,1},{1,0},{2,3},{3,2},{4,5},{5,4},{6,7},{7,6},{8,9},{9,8},{10,11... | collective-permute-start | bytes 2696 | tf_op jit(solution)/shard_map/ppermute | solution.py:21
  1.7 10.6 %collective-permute-start = (bf16[4,3584]{1,0:T(4,128)(2,1)}, bf16[4,3584]{1,0:T(4,128)(2,1)S(1)}, u32[]{:S(2)}, u32[]{:S(2)}) collective-permute-start(bf16[4,3584]{1,0:T(4,128)(2,1)} %resid_hbm.1), channel_id=1, source_target_pairs={{0,3},{1,2},{2,1},{3,0},{4,7},{5,6},{6,5},{7,4},{8,11},{9,10},{10,... | collective-permute-start | bytes 86024 | tf_op jit(solution)/shard_map/ppermute | solution.py:21
  4.3 8.0 %collective-permute-start.1 = (bf16[4,3584]{1,0:T(4,128)(2,1)}, bf16[4,3584]{1,0:T(4,128)(2,1)S(1)}, u32[]{:S(2)}, u32[]{:S(2)}) collective-permute-start(bf16[4,3584]{1,0:T(4,128)(2,1)} %resid_hbm.1), channel_id=1, source_target_pairs={{0,5},{1,4},{2,7},{3,6},{4,1},{5,0},{6,3},{7,2},{8,13},{9,12},{10,... | collective-permute-start | bytes 86024 | tf_op jit(solution)/shard_map/ppermute | solution.py:21
  6.8 5.5 %collective-permute-start.2 = (bf16[4,3584]{1,0:T(4,128)(2,1)}, bf16[4,3584]{1,0:T(4,128)(2,1)S(1)}, u32[]{:S(2)}, u32[]{:S(2)}) collective-permute-start(bf16[4,3584]{1,0:T(4,128)(2,1)} %resid_hbm.1), channel_id=1, source_target_pairs={{0,7},{1,6},{2,5},{3,4},{4,3},{5,2},{6,1},{7,0},{8,15},{9,14},{10,... | collective-permute-start | bytes 86024 | tf_op jit(solution)/shard_map/ppermute | solution.py:21
  13.8 4.0 %collective-permute-start.6 = (f32[4,3584]{1,0:T(4,128)S(1)}, f32[4,3584]{1,0:T(4,128)S(1)}, u32[]{:S(2)}, u32[]{:S(2)}) collective-permute-start(f32[4,3584]{1,0:T(4,128)S(1)} %get-tuple-element.30), channel_id=1, source_target_pairs={{0,3},{1,2},{2,1},{3,0},{4,7},{5,6},{6,5},{7,4},{8,11},{9,10},{10,... | collective-permute-start | bytes 172040 | tf_op jit(solution)/shard_map/ppermute | solution.py:21
  15.3 3.7 %collective-permute-start.7 = (f32[4,3584]{1,0:T(4,128)S(1)}, f32[4,3584]{1,0:T(4,128)S(1)}, u32[]{:S(2)}, u32[]{:S(2)}) collective-permute-start(f32[4,3584]{1,0:T(4,128)S(1)} %get-tuple-element.31), channel_id=1, source_target_pairs={{0,5},{1,4},{2,7},{3,6},{4,1},{5,0},{6,3},{7,2},{8,13},{9,12},{10,... | collective-permute-start | bytes 172040 | tf_op jit(solution)/shard_map/ppermute | solution.py:21
  16.8 4.8 %collective-permute-start.8 = (f32[4,3584]{1,0:T(4,128)S(1)}, f32[4,3584]{1,0:T(4,128)S(1)}, u32[]{:S(2)}, u32[]{:S(2)}) collective-permute-start(f32[4,3584]{1,0:T(4,128)S(1)} %get-tuple-element.32), channel_id=1, source_target_pairs={{0,7},{1,6},{2,5},{3,4},{4,3},{5,2},{6,1},{7,0},{8,15},{9,14},{10,... | collective-permute-start | bytes 172040 | tf_op jit(solution)/shard_map/ppermute | solution.py:21
  17.1 8.8 %copy-start = (f32[3584]{0:T(1024)S(1)}, f32[3584]{0:T(1024)}, u32[]{:S(2)}) copy-start(f32[3584]{0:T(1024)} %param.9) | copy-start | bytes 43012
  21.6 6.7 %collective-permute-start.10 = (f32[4,3712]{1,0:T(4,128)S(1)}, f32[4,3712]{1,0:T(4,128)S(1)}, u32[]{:S(2)}, u32[]{:S(2)}) collective-permute-start(f32[4,3712]{1,0:T(4,128)S(1)} %shard_map.95.refs_0_), channel_id=1, source_target_pairs={{0,16},{8,24},{16,0},{24,8},{1,17},{9,25},{17,1},{25,9},{2,18},{10... | collective-permute-start | bytes 178184 | tf_op jit(solution)/shard_map/ppermute | solution.py:21
  24.3 6.2 %collective-permute-start.11 = (f32[4,3712]{1,0:T(4,128)S(1)}, f32[4,3712]{1,0:T(4,128)S(1)}, u32[]{:S(2)}, u32[]{:S(2)}) collective-permute-start(f32[4,3712]{1,0:T(4,128)S(1)} %shard_map.95.refs_0_), channel_id=1, source_target_pairs={{0,24},{8,16},{16,8},{24,0},{1,25},{9,17},{17,9},{25,1},{2,26},{10... | collective-permute-start | bytes 178184 | tf_op jit(solution)/shard_map/ppermute | solution.py:21
  25.6 5.0 %collective-permute-start.9 = (f32[4,3712]{1,0:T(4,128)S(1)}, f32[4,3712]{1,0:T(4,128)S(1)}, u32[]{:S(2)}, u32[]{:S(2)}) collective-permute-start(f32[4,3712]{1,0:T(4,128)S(1)} %shard_map.95.refs_0_), channel_id=1, source_target_pairs={{0,8},{8,0},{16,24},{24,16},{1,9},{9,1},{17,25},{25,17},{2,10},{10... | collective-permute-start | bytes 178184 | tf_op jit(solution)/shard_map/ppermute | solution.py:21
  30.7 3.5 %collective-permute-start.12 = (bf16[8,2816]{1,0:T(8,128)(2,1)S(1)}, bf16[8,2816]{1,0:T(8,128)(2,1)S(1)}, u32[]{:S(2)}, u32[]{:S(2)}) collective-permute-start(bf16[8,2816]{1,0:T(8,128)(2,1)S(1)} %shard_map.97.refs_0_), channel_id=1, source_target_pairs={{0,3},{1,2},{2,1},{3,0},{4,7},{5,6},{6,5},{7,4},{8,11},{9,10},{10,... | collective-permute-start | bytes 135176 | tf_op jit(solution)/shard_map/ppermute | solution.py:21
  30.8 3.5 %collective-permute-start.13 = (bf16[8,2816]{1,0:T(8,128)(2,1)S(1)}, bf16[8,2816]{1,0:T(8,128)(2,1)S(1)}, u32[]{:S(2)}, u32[]{:S(2)}) collective-permute-start(bf16[8,2816]{1,0:T(8,128)(2,1)S(1)} %shard_map.97.refs_0_), channel_id=1, source_target_pairs={{0,5},{1,4},{2,7},{3,6},{4,1},{5,0},{6,3},{7,2},{8,13},{9,12},{10,... | collective-permute-start | bytes 135176 | tf_op jit(solution)/shard_map/ppermute | solution.py:21
  31.4 4.6 %collective-permute-start.14 = (bf16[8,2816]{1,0:T(8,128)(2,1)S(1)}, bf16[8,2816]{1,0:T(8,128)(2,1)S(1)}, u32[]{:S(2)}, u32[]{:S(2)}) collective-permute-start(bf16[8,2816]{1,0:T(8,128)(2,1)S(1)} %shard_map.97.refs_0_), channel_id=1, source_target_pairs={{0,7},{1,6},{2,5},{3,4},{4,3},{5,2},{6,1},{7,0},{8,15},{9,14},{10,... | collective-permute-start | bytes 135176 | tf_op jit(solution)/shard_map/ppermute | solution.py:21
  32.6 6.2 %collective-permute-start.15 = (bf16[8,2816]{1,0:T(8,128)(2,1)S(1)}, bf16[8,2816]{1,0:T(8,128)(2,1)S(1)}, u32[]{:S(2)}, u32[]{:S(2)}) collective-permute-start(bf16[8,2816]{1,0:T(8,128)(2,1)S(1)} %shard_map.97.refs_0_), channel_id=1, source_target_pairs={{0,1},{1,0},{2,3},{3,2},{4,5},{5,4},{6,7},{7,6},{8,9},{9,8},{10,11... | collective-permute-start | bytes 135176 | tf_op jit(solution)/shard_map/ppermute | solution.py:21
  34.3 4.5 %collective-permute-start.16 = (bf16[8,2816]{1,0:T(8,128)(2,1)S(1)}, bf16[8,2816]{1,0:T(8,128)(2,1)S(1)}, u32[]{:S(2)}, u32[]{:S(2)}) collective-permute-start(bf16[8,2816]{1,0:T(8,128)(2,1)S(1)} %collective-permute-done.12.refs_1_), channel_id=1, source_target_pairs={{0,1},{1,0},{2,3},{3,2},{4,5},{5,4},{6,7},{7,6},{8,9},{9,8},{10,11... | collective-permute-start | bytes 135176 | tf_op jit(solution)/shard_map/ppermute | solution.py:21
  34.4 4.4 %collective-permute-start.17 = (bf16[8,2816]{1,0:T(8,128)(2,1)S(1)}, bf16[8,2816]{1,0:T(8,128)(2,1)S(1)}, u32[]{:S(2)}, u32[]{:S(2)}) collective-permute-start(bf16[8,2816]{1,0:T(8,128)(2,1)S(1)} %collective-permute-done.13.refs_2_), channel_id=1, source_target_pairs={{0,1},{1,0},{2,3},{3,2},{4,5},{5,4},{6,7},{7,6},{8,9},{9,8},{10,11... | collective-permute-start | bytes 135176 | tf_op jit(solution)/shard_map/ppermute | solution.py:21
  36.0 2.8 %collective-permute-start.18 = (bf16[8,2816]{1,0:T(8,128)(2,1)S(1)}, bf16[8,2816]{1,0:T(8,128)(2,1)S(1)}, u32[]{:S(2)}, u32[]{:S(2)}) collective-permute-start(bf16[8,2816]{1,0:T(8,128)(2,1)S(1)} %collective-permute-done.14.refs_3_), channel_id=1, source_target_pairs={{0,1},{1,0},{2,3},{3,2},{4,5},{5,4},{6,7},{7,6},{8,9},{9,8},{10,11... | collective-permute-start | bytes 135176 | tf_op jit(solution)/shard_map/ppermute | solution.py:21
  36.1 1.2 %collective-permute-start.19 = (bf16[16,224]{1,0:T(8,128)(2,1)S(1)}, bf16[16,224]{1,0:T(8,128)(2,1)S(1)}, u32[]{:S(2)}, u32[]{:S(2)}) collective-permute-start(bf16[16,224]{1,0:T(8,128)(2,1)S(1)} %get-tuple-element.34.codes2_ref), channel_id=1, source_target_pairs={{0,1},{1,0},{2,3},{3,2},{4,5},{5,4},{6,7},{7,6},{8,9},{9,8},{10,11... | collective-permute-start | bytes 21512 | tf_op jit(solution)/shard_map/ppermute | solution.py:21
